TPU v7x, 256 devices: a whole 4x4x8 slice. The times are simulated.
256 devices in a mesh: rows: 8 (over x, core), protos: 32 (over y, z).
Axes of the slice: x: 4, y: 4, z: 8, core: 2. Of those that a mesh axis runs over, the one named last changes fastest.
Arguments:
- teacher_features: bfloat16 [4096, 384], P(('rows', 'protos')), may hold values from -80 to 80, as said below
- student_features: bfloat16 [4096, 384], P(('rows', 'protos')), may hold values from -80 to 80, as said below
- prototypes: bfloat16 [131072, 384], P('protos'), may hold values from -80 to 80, as said below
Outputs:
- feature_grad: float32 [4096, 384], P(('rows', 'protos'))
- proto_grad: float32 [8, 16384, 384], P('rows', 'protos')
Inputs may be any that keep to these rules, and one draw needn't show every extreme that they name: `teacher_features`: every row has nonzero entries. `student_features`: every row has nonzero entries. `prototypes`: every row has nonzero entries.
All inputs are finite; a program needn't handle non-finite values.
Results may differ from a plain program's by a relative error of at most 0.012.
The roundings to bfloat16 on the way count: a program that leaves them out, or rounds other values in their place, can miss the bound.
Values may be sent and summed in bfloat16 or wider, within the bound.
A program may use at most 64 MiB of HBM per device.

v0:
```python
import math

import jax
import jax.numpy as jnp
from jax import lax
from jax.sharding import PartitionSpec as P

D = 384
K = 131072
PASSES = 3


eps = 1e-06


def unitize(values):
    values = values.astype(jnp.float32)
    return (values * lax.rsqrt(jnp.sum(values * values, axis=1, keepdims=True) + eps)).astype(
        jnp.bfloat16
    )


def against(left, right):
    return lax.dot_general(
        left, right, (((1,), (1,)), ((), ())), preferred_element_type=jnp.float32
    )


def on_device(teacher_features, student_features, prototypes):
    scale = 1.5 * math.sqrt(D)
    unit_w = unitize(prototypes)
    local_t = unitize(teacher_features)
    local_s = unitize(student_features)
    unit_t, unit_s = (
        lax.all_gather(local_t, "protos", axis=0, tiled=True),
        lax.all_gather(local_s, "protos", axis=0, tiled=True),
    )
    kernel = jnp.exp(scale * against(unit_t, unit_w))
    powers = jnp.exp(scale * against(unit_s, unit_w))
    student_part = jnp.sum(powers, axis=1)
    student_whole = lax.psum(student_part, "protos")
    row_scale = jnp.ones((kernel.shape[0],), jnp.float32)
    col_scale = jnp.ones((kernel.shape[1],), jnp.float32)
    for step in range(PASSES):
        col_part = jnp.dot(row_scale, kernel, precision=lax.Precision.HIGHEST)
        col_scale = 1.0 / lax.psum(col_part, "rows")
        row_part = jnp.dot(kernel, col_scale, precision=lax.Precision.HIGHEST)
        if step == 0:
            row_whole = lax.psum(row_part, "protos")
        else:
            row_whole = lax.psum(row_part, "protos")
        row_scale = 1.0 / row_whole
    target = kernel * row_scale[:, None] * col_scale[None, :]
    probs = powers / student_whole[:, None]
    delta = (probs - target).astype(jnp.bfloat16)
    feature_term = scale * jnp.dot(delta, unit_w, preferred_element_type=jnp.float32)
    feature_grad = lax.psum_scatter(feature_term, "protos", scatter_dimension=0, tiled=True)
    row_groups = lax.axis_size("rows")
    total_rows = delta.shape[0] * row_groups
    factor = scale * K / total_rows
    block = delta.shape[1] // row_groups
    term = factor * lax.dot_general(
        delta, unit_s, (((0,), (0,)), ((), ())), preferred_element_type=jnp.float32
    )
    proto_grad = lax.psum_scatter(
        term.reshape(row_groups, block, term.shape[1]), "rows", scatter_dimension=0, tiled=True
    )
    return (feature_grad, proto_grad)


def solution(mesh):
    return jax.shard_map(
        on_device,
        mesh=mesh,
        in_specs=(P(("rows", "protos"), None), P(("rows", "protos"), None), P("protos", None)),
        out_specs=(P(("rows", "protos"), None), P("rows", "protos", None)),
        check_vma=False,
    )
```

profile of v0, /device:TPU:1, one launch (start us, length us, event | category | flops | bytes accessed | tf_op | source)
XLA Modules:
  0.0 735.6 jit_solution(5828482277272511359)
XLA Ops:
  7.2 0.0 reduce-scatter.3.cloned.1.call-start
  7.2 0.8 fusion.5
  8.0 0.8 fusion.3
  8.9 0.8 fusion.4
  9.7 0.8 fusion.6
  10.4 2.6 fusion.1
  13.1 41.6 %all_gather.6 = bf16[512,384]{1,0:T(8,128)(2,1)S(1)} all-gather(bf16[16,384]{1,0:T(8,128)(2,1)S(1)} %fusion.4), channel_id=1, replica_groups=mesh['rows'=8,'protos'=32] {'protos'}, dimensions={0}, use_global_device_ids=true | all-gather | bytes 405504 | tf_op jit(solution)/shard_map/all_gather | solution.py:36
  54.6 36.7 %all_gather.7 = bf16[512,384]{1,0:T(8,128)(2,1)S(1)} all-gather(bf16[16,384]{1,0:T(8,128)(2,1)S(1)} %fusion.6), channel_id=1, replica_groups=mesh['rows'=8,'protos'=32] {'protos'}, dimensions={0}, use_global_device_ids=true | all-gather | bytes 405504 | tf_op jit(solution)/shard_map/all_gather | solution.py:35
  91.3 4.3 multiply_exponential_fusion
  95.7 3.2 copy-done
  98.9 4.0 fusion.7
  102.9 44.7 %psum.50 = f32[4096]{0:T(1024)S(1)} all-reduce(f32[4096]{0:T(1024)S(1)} %bitcast.34), channel_id=1, replica_groups=mesh['rows'=8,'protos'=32] {'rows'}, use_global_device_ids=true, to_apply=%region_5.0 | all-reduce | flops 4096 | bytes 32768 | tf_op jit(solution)/shard_map/psum | solution.py:46
  147.7 9.4 %fusion.14 = f32[1,512]{1,0:T(1,128)S(1)} fusion(f32[512,4096]{1,0:T(8,128)} %copy-done, f32[4096,1]{0,1:T(1,128)S(1)} %bitcast.30), kind=kOutput, calls=%fused_computation.31 | convolution fusion | flops 25165824 | bytes 8407040 | tf_op jit(solution)/shard_map/dot_general | solution.py:47
  157.1 58.6 %psum.51 = f32[512]{0:T(512)S(1)} all-reduce(f32[512]{0:T(512)S(1)} %bitcast.36), channel_id=1, replica_groups=mesh['rows'=8,'protos'=32] {'protos'}, use_global_device_ids=true, to_apply=%region_6.0 | all-reduce | flops 512 | bytes 4096 | tf_op jit(solution)/shard_map/psum | solution.py:49
  215.7 6.3 fusion.15
  222.1 37.4 %psum.52 = f32[4096]{0:T(1024)S(1)} all-reduce(f32[4096]{0:T(1024)S(1)} %bitcast.31), channel_id=1, replica_groups=mesh['rows'=8,'protos'=32] {'rows'}, use_global_device_ids=true, to_apply=%region_7.0 | all-reduce | flops 4096 | bytes 32768 | tf_op jit(solution)/shard_map/psum | solution.py:46
  259.5 9.4 %fusion.16 = f32[1,512]{1,0:T(1,128)S(1)} fusion(f32[512,4096]{1,0:T(8,128)} %copy-done, f32[4096,1]{0,1:T(1,128)S(1)} %bitcast.32), kind=kOutput, calls=%fused_computation.33 | convolution fusion | flops 25165824 | bytes 8407040 | tf_op jit(solution)/shard_map/dot_general | solution.py:47
  268.9 55.8 %psum.53 = f32[512]{0:T(512)S(1)} all-reduce(f32[512]{0:T(512)S(1)} %bitcast.38), channel_id=1, replica_groups=mesh['rows'=8,'protos'=32] {'protos'}, use_global_device_ids=true, to_apply=%region_8.0 | all-reduce | flops 512 | bytes 4096 | tf_op jit(solution)/shard_map/psum | solution.py:51
  324.7 6.5 fusion.17
  331.2 37.6 %psum.54 = f32[4096]{0:T(1024)} all-reduce(f32[4096]{0:T(1024)S(1)} %bitcast.33), channel_id=1, replica_groups=mesh['rows'=8,'protos'=32] {'rows'}, use_global_device_ids=true, to_apply=%region_9.0 | all-reduce | flops 4096 | bytes 32768 | tf_op jit(solution)/shard_map/psum | solution.py:46
  368.8 0.7 broadcast_divide_fusion
  369.6 10.0 %fusion.18 = f32[1,512]{1,0:T(1,128)} fusion(f32[512,4096]{1,0:T(8,128)} %copy-done, f32[4096,1]{0,1:T(1,128)S(1)} %bitcast.29), kind=kOutput, calls=%fused_computation.35 | convolution fusion | flops 25165824 | bytes 8407040 | tf_op jit(solution)/shard_map/dot_general | solution.py:47
  379.6 6.2 fusion
  385.8 58.2 %all-reduce = (f32[512]{0:T(512)}, f32[512]{0:T(512)}) all-reduce(f32[512]{0:T(512)} %bitcast.35, f32[512]{0:T(512)} %get-tuple-element.4), channel_id=1, replica_groups=mesh['rows'=8,'protos'=32] {'protos'}, use_global_device_ids=true, to_apply=%region_10.0 | all-reduce | flops 1024 | bytes 8192 | tf_op jit(solution)/shard_map/psum | solution.py:51
  444.0 0.7 broadcast_divide_fusion.5
  444.6 7.3 subtract_convert_fusion
  452.0 2.0 copy-done.2
  454.0 3.3 convolution_multiply_fusion.1
  457.4 0.0 reduce-scatter.5.cloned.1.call-start
  457.4 7.2 convolution_multiply_fusion
  464.7 212.9 %reduce-scatter.3.cloned.1.call-done = f32[16,384]{1,0:T(8,128)} async-done(((f32[512,384]{1,0:T(8,128)}), f32[16,384]{1,0:T(8,128)}) %reduce-scatter.3.cloned.1.call-update) | async-done | bytes 24592 | tf_op jit(solution)/shard_map/reduce_scatter | solution.py:57
  677.6 51.2 %reduce-scatter.5.cloned.1.call-done = f32[1,512,384]{2,1,0:T(8,128)} async-done(((f32[8,512,384]{2,1,0:T(8,128)}), f32[1,512,384]{2,1,0:T(8,128)}) %reduce-scatter.5.cloned.1.call-update) | async-done | bytes 786448 | tf_op jit(solution)/shard_map/reduce_scatter | solution.py:65
  (17 shorter events, 0.1 us)
Async XLA Ops:
  7.2 670.4 %reduce-scatter.3.cloned.1.call-start = ((), (), s32[]{:S(2)}) async-start(), calls=%async_computation.2 | async-start | bytes 811008 | tf_op jit(solution)/shard_map/reduce_scatter | solution.py:57
  13.0 89.9 %copy-start.3 = (f32[4096]{0:T(1024)}, f32[4096]{0:T(1024)S(1)}, u32[]{:S(2)}) copy-start(f32[4096]{0:T(1024)S(1)} %add_rsqrt_fusion) | copy-start | bytes 49156
  95.7 3.2 copy-start
  324.7 54.9 %copy-start.1 = (bf16[4096,384]{1,0:T(8,128)(2,1)S(1)}, bf16[4096,384]{1,0:T(8,128)(2,1)}, u32[]{:S(2)}) copy-start(bf16[4096,384]{1,0:T(8,128)(2,1)} %param.5) | copy-start | bytes 9437188
  444.6 9.4 %copy-start.4 = (f32[4096]{0:T(1024)S(1)}, f32[4096]{0:T(1024)}, u32[]{:S(2)}) copy-start(f32[4096]{0:T(1024)} %copy-done.3) | copy-start | bytes 49156
  452.0 2.0 copy-start.2
  457.4 271.4 %reduce-scatter.5.cloned.1.call-start = ((), (), s32[]{:S(2)}) async-start(), calls=%async_computation.3 | async-start | bytes 7077888 | tf_op jit(solution)/shard_map/reduce_scatter | solution.py:65
Sparse Core Ops, SparseCore 0:
  457.5 220.0 reduce-scatter.2
  680.7 48.0 reduce-scatter.4
where the time goes:
time: 736 us
  blocking collectives  371 us (50%)
  waiting for transfers between devices  264 us (36%)
  matrix products  66.9 us (9%)
  other arithmetic  14.6 us (2%)
  between operations  14.1 us (2%)
    reduce_scatter x1, waiting for transfers between devices, on_device(): lax.psum_scatter(feature_term, 'protos', scatter_dimension=0, tiled=True)  213 us
    psum x3, blocking collectives, on_device(): row_whole = lax.psum(row_part, 'protos')  173 us
    psum x3, blocking collectives, on_device(): col_scale = 1.0 / lax.psum(col_part, 'rows')  120 us
    reduce_scatter x1, waiting for transfers between devices, on_device(): lax.psum_scatter(term.reshape(row_groups, block, term.shape[1]), 'rows',...  51.2 us
    all_gather x1, blocking collectives, on_device(): lax.all_gather(local_s, 'protos', axis=0, tiled=True)  41.6 us
    all_gather x1, blocking collectives, on_device(): lax.all_gather(local_t, 'protos', axis=0, tiled=True)  36.7 us
    dot_general x3, matrix products, on_device(): row_part = jnp.dot(kernel, col_scale, precision=lax.Precision.HIGHEST)  28.9 us
    dot_general x3, matrix products, on_device(): col_part = jnp.dot(row_scale, kernel, precision=lax.Precision.HIGHEST)  16.9 us
  transfers between devices with their start and end apart: 2, of which 2 were waited for; matrix products, arithmetic and copies ran while one was open for 1% of the time, Pallas kernels for 0%

commit v1 on v0

v1 whole, which is shorter than its diff:
```python
import functools
import math

import jax
import jax.numpy as jnp
from jax import lax
from jax.experimental import pallas as pl
from jax.experimental.pallas import tpu as pltpu
from jax.sharding import PartitionSpec as P

K = 131072
PASSES = 3
EPS = 1e-06
LANES = 128
STEP = 256
CHIPS = 4
MESH = pl.DeviceIdType.MESH
f32 = jnp.float32
bf16 = jnp.bfloat16


def unitize(values):
    values = values.astype(f32)
    return (values * lax.rsqrt(jnp.sum(values * values, axis=1, keepdims=True) + EPS)).astype(bf16)


def kernel(
    n_rows, n_protos, factor_rows,
    t_ref, s_ref, w_ref, fg_ref, pg_ref,
    tg, sg, uw, km, pm, st, rb, qb, acc, cbuf, cvec, rbuf, qbuf,
    dbuf, feat, fsend, frecv, psend, precv, xsend, relay, xrecv, hold, own,
    t_ss, t_rs, s_ss, s_rs, c_ss, c_rs, r_ss, r_rs, q_ss, q_rs,
    p_ss, p_rs, x_ss, l_rs, x_rs, f_ss, f_rs,
):
    rows, protos = km.shape
    depth = uw.shape[1]
    block = t_ref.shape[0]
    chunk = protos // n_rows
    half = chunk // 2
    scale = 1.5 * math.sqrt(depth)
    power = scale * math.log2(math.e)
    factor = scale * K / factor_rows
    r = lax.axis_index("rows")
    p = lax.axis_index("protos")

    barrier = pltpu.get_barrier_semaphore()

    def greet(axis, me, count):
        def one(k, _):
            pl.semaphore_signal(
                barrier, inc=1, device_id={axis: lax.rem(me + k, count)}, device_id_type=MESH
            )
            return 0

        lax.fori_loop(1, count, one, 0)

    greet("protos", p, n_protos)
    greet("rows", r, n_rows)

    def spread(axis, me, count, source, target, send_sem, recv_sem):
        def one(k, _):
            pltpu.make_async_remote_copy(
                src_ref=source,
                dst_ref=target,
                send_sem=send_sem,
                recv_sem=recv_sem,
                device_id={axis: lax.rem(me + k, count)},
                device_id_type=MESH,
            ).start()
            return 0

        lax.fori_loop(1, count, one, 0)

    def drain(view, sem):
        pltpu.make_async_copy(view, view, sem).wait()

    tg[p] = unitize(t_ref[...])
    sg[p] = unitize(s_ref[...])
    pl.semaphore_wait(barrier, n_protos + n_rows - 2)
    spread("protos", p, n_protos, tg.at[p], tg.at[p], t_ss, t_rs)
    spread("protos", p, n_protos, sg.at[p], sg.at[p], s_ss, s_rs)

    def unit_step(i, _):
        at = pl.ds(pl.multiple_of(i * STEP, STEP), STEP)
        uw[at, :] = unitize(w_ref[at, :])
        return 0

    lax.fori_loop(0, protos // STEP, unit_step, 0)

    others = pl.ds(0, n_protos - 1)
    drain(tg.at[others], t_rs)

    def logits(left, i):
        at = pl.ds(pl.multiple_of(i * STEP, STEP), STEP)
        values = lax.dot_general(
            left, uw[at, :], (((1,), (1,)), ((), ())), preferred_element_type=f32
        )
        return at, jnp.exp2(values * power)

    teacher = tg[...].reshape(rows, depth)

    def kernel_step(i, _):
        at, values = logits(teacher, i)
        km[:, at] = values
        cbuf[0, r, :, at] = jnp.sum(values, axis=0, keepdims=True)
        return 0

    lax.fori_loop(0, protos // STEP, kernel_step, 0)

    def column(values):
        return jnp.transpose(jnp.broadcast_to(values, (LANES, LANES)))

    def to_columns(values, ref):
        for g in range(rows // LANES):
            ref[g * LANES:(g + 1) * LANES, :] = column(values[:, g * LANES:(g + 1) * LANES])

    def lane_sums(store):
        for g in range(rows // LANES):
            turned = jnp.transpose(acc[g * LANES:(g + 1) * LANES, :])
            store(slice(g * LANES, (g + 1) * LANES), jnp.sum(turned, axis=0, keepdims=True))

    tiles = protos // LANES

    def lane(j):
        return slice(j * LANES, (j + 1) * LANES)

    def column_pass(step):
        def one(i, sums):
            at = pl.ds(pl.multiple_of(i * 8, 8), 8)
            value = rb[at, :]
            return tuple(sums[j] + km[at, lane(j)] * value for j in range(tiles))

        sums = lax.fori_loop(
            0, rows // 8, one, tuple(jnp.zeros((8, LANES), f32) for _ in range(tiles)), unroll=2
        )
        for j in range(tiles):
            cbuf[step, r, :, lane(j)] = jnp.sum(sums[j], axis=0, keepdims=True)

    def row_pass(step):
        cols = [jnp.broadcast_to(cvec[:, lane(j)], (8, LANES)) for j in range(tiles)]

        def one(i, _):
            at = pl.ds(pl.multiple_of(i * 8, 8), 8)
            parts = [km[at, lane(j)] * cols[j] for j in range(4)]
            for j in range(4, tiles):
                parts[j % 4] = parts[j % 4] + km[at, lane(j)] * cols[j]
            acc[at, :] = (parts[0] + parts[1]) + (parts[2] + parts[3])
            return 0

        lax.fori_loop(0, rows // 8, one, 0, unroll=2)

        def store(at, value):
            rbuf[step, p, :, at] = value

        lane_sums(store)

    def student():
        drain(sg.at[others], s_rs)
        units = sg[...].reshape(rows, depth)
        acc[...] = jnp.zeros_like(acc)

        def one(i, _):
            at, values = logits(units, i)
            pm[:, at] = values
            acc[...] += values[:, :LANES] + values[:, LANES:]
            return 0

        lax.fori_loop(0, protos // STEP, one, 0)

        def store(at, value):
            qbuf[p, :, at] = value

        lane_sums(store)
        spread("protos", p, n_protos, qbuf.at[p], qbuf.at[p], q_ss, q_rs)
        st[...] = jnp.transpose(units.astype(f32)).astype(bf16)

    for step in range(PASSES):
        if step > 0:
            column_pass(step)
        spread(
            "rows", r, n_rows, cbuf.at[step, r], cbuf.at[step, r], c_ss.at[step], c_rs.at[step]
        )
        if step == 1:
            drain(qbuf.at[others], q_rs)
            to_columns(1.0 / jnp.sum(qbuf[...], axis=0), qb)
        drain(cbuf.at[step, pl.ds(0, n_rows - 1)], c_rs.at[step])
        cvec[...] = 1.0 / jnp.sum(cbuf[step], axis=0)
        row_pass(step)
        spread(
            "protos", p, n_protos, rbuf.at[step, p], rbuf.at[step, p], r_ss.at[step], r_rs.at[step]
        )
        if step == 0:
            student()
        drain(rbuf.at[step, others], r_rs.at[step])
        to_columns(1.0 / jnp.sum(rbuf[step], axis=0), rb)

    def term(owner, first):
        at = pl.ds(pl.multiple_of(owner * chunk, chunk), chunk)
        cols = cvec[:, at]

        def one(i, _):
            here = pl.ds(pl.multiple_of(i * 16, 16), 16)
            row = jnp.concatenate([rb[here, :]] * (chunk // LANES), axis=1)
            inv = jnp.concatenate([qb[here, :]] * (chunk // LANES), axis=1)
            delta = pm[here, at] * inv - km[here, at] * row * cols
            dbuf[here, :] = delta.astype(bf16)
            return 0

        lax.fori_loop(0, rows // 16, one, 0, unroll=2)
        delta = dbuf[...]
        part = jnp.dot(delta, uw[at, :], preferred_element_type=f32)
        if first:
            feat[...] = part
        else:
            feat[...] += part
        return jnp.dot(st[...], delta, preferred_element_type=f32)

    x, core = lax.div(r, 2), lax.rem(r, 2)

    def send(source, target, send_sem, recv_sem, to):
        pltpu.make_async_remote_copy(
            src_ref=source, dst_ref=target, send_sem=send_sem, recv_sem=recv_sem,
            device_id={"rows": to}, device_id_type=MESH,
        ).start()

    up = lax.rem(x + 1, CHIPS) * 2 + core
    down = lax.rem(x + CHIPS - 1, CHIPS) * 2 + core
    mate = x * 2 + 1 - core

    for k, ahead in enumerate((2, 1, 3, 0)):
        chip = lax.rem(x + ahead, CHIPS)
        part = term(chip * 2 + 1 - core, k == 0)
        psend[k, 0] = part[:, :half].astype(bf16)
        psend[k, 1] = part[:, half:].astype(bf16)
        send(psend.at[k], precv.at[k], p_ss.at[k], p_rs.at[k], mate)
        part = term(chip * 2 + core, False)
        drain(precv.at[k], p_rs.at[k])
        low = part[:, :half] + precv[k, 0].astype(f32)
        high = part[:, half:] + precv[k, 1].astype(f32)
        if k == 0:
            xsend[0, 0] = low.astype(bf16)
            xsend[0, 1] = high.astype(bf16)
            send(xsend.at[0, 0], relay.at[0], x_ss.at[0, 0], l_rs.at[0], up)
            send(xsend.at[0, 1], relay.at[1], x_ss.at[0, 1], l_rs.at[1], down)
        elif k == 1:
            hold[0] = low
            xsend[1, 1] = high.astype(bf16)
            send(xsend.at[1, 1], xrecv.at[0, 1], x_ss.at[1, 1], x_rs.at[0, 1], up)
        elif k == 2:
            hold[1] = high
            xsend[2, 0] = low.astype(bf16)
            send(xsend.at[2, 0], xrecv.at[1, 0], x_ss.at[2, 0], x_rs.at[1, 0], down)
        else:
            own[0] = low
            own[1] = high

    def feature_step(i, _):
        at = pl.ds(pl.multiple_of(i * block, block), block)
        fsend[i] = feat[at, :].astype(bf16)
        return 0

    lax.fori_loop(0, n_protos, feature_step, 0)

    def feature_send(k, _):
        q = lax.rem(p + k, n_protos)
        pltpu.make_async_remote_copy(
            src_ref=fsend.at[q], dst_ref=frecv.at[p], send_sem=f_ss, recv_sem=f_rs,
            device_id={"protos": q}, device_id_type=MESH,
        ).start()
        return 0

    lax.fori_loop(1, n_protos, feature_send, 0)
    frecv[p] = fsend[p]

    drain(relay.at[0], l_rs.at[0])
    xsend[1, 0] = (hold[0] + relay[0].astype(f32)).astype(bf16)
    send(xsend.at[1, 0], xrecv.at[0, 0], x_ss.at[1, 0], x_rs.at[0, 0], up)
    drain(relay.at[1], l_rs.at[1])
    xsend[2, 1] = (hold[1] + relay[1].astype(f32)).astype(bf16)
    send(xsend.at[2, 1], xrecv.at[1, 1], x_ss.at[2, 1], x_rs.at[1, 1], down)

    drain(frecv.at[others], f_rs)
    total = jnp.zeros((block, depth), f32)
    total = lax.fori_loop(0, n_protos, lambda i, a: a + frecv[i].astype(f32), total)
    fg_ref[...] = scale * total

    for side in range(2):
        for h in range(2):
            drain(xrecv.at[side, h], x_rs.at[side, h])
    for h in range(2):
        whole = own[h] + xrecv[0, h].astype(f32) + xrecv[1, h].astype(f32)
        pg_ref[h * half:(h + 1) * half, :] = jnp.transpose(factor * whole)

    drain(tg.at[others], t_ss)
    drain(sg.at[others], s_ss)
    drain(qbuf.at[others], q_ss)
    drain(frecv.at[others], f_ss)
    for step in range(PASSES):
        drain(cbuf.at[step, pl.ds(0, n_rows - 1)], c_ss.at[step])
        drain(rbuf.at[step, others], r_ss.at[step])
    for k in range(4):
        drain(psend.at[k], p_ss.at[k])
    for k in range(3):
        for h in range(2):
            drain(xsend.at[k, h], x_ss.at[k, h])


def on_device(teacher_features, student_features, prototypes):
    n_rows, n_protos = lax.axis_size("rows"), lax.axis_size("protos")
    block, depth = teacher_features.shape
    protos = prototypes.shape[0]
    rows = block * n_protos
    chunk = protos // n_rows
    half = chunk // 2
    dma = pltpu.SemaphoreType.DMA
    vmem = pltpu.VMEM
    feature_grad, proto_grad = pl.pallas_call(
        functools.partial(kernel, n_rows, n_protos, rows * n_rows),
        out_shape=(
            jax.ShapeDtypeStruct((block, depth), f32),
            jax.ShapeDtypeStruct((chunk, depth), f32),
        ),
        in_specs=[pl.BlockSpec(memory_space=pltpu.VMEM)] * 3,
        out_specs=(pl.BlockSpec(memory_space=pltpu.VMEM),) * 2,
        scratch_shapes=[
            vmem((n_protos, block, depth), bf16),
            vmem((n_protos, block, depth), bf16),
            vmem((protos, depth), bf16),
            vmem((rows, protos), f32),
            vmem((rows, protos), f32),
            vmem((depth, rows), bf16),
            vmem((rows, LANES), f32),
            vmem((rows, LANES), f32),
            vmem((rows, LANES), f32),
            vmem((PASSES, n_rows, 1, protos), f32),
            vmem((1, protos), f32),
            vmem((PASSES, n_protos, 1, rows), f32),
            vmem((n_protos, 1, rows), f32),
            vmem((rows, chunk), bf16),
            vmem((rows, depth), f32),
            vmem((n_protos, block, depth), bf16),
            vmem((n_protos, block, depth), bf16),
            vmem((4, 2, depth, half), bf16),
            vmem((4, 2, depth, half), bf16),
            vmem((3, 2, depth, half), bf16),
            vmem((2, depth, half), bf16),
            vmem((2, 2, depth, half), bf16),
            vmem((2, depth, half), f32),
            vmem((2, depth, half), f32),
            dma, dma, dma, dma,
            dma((PASSES,)), dma((PASSES,)), dma((PASSES,)), dma((PASSES,)),
            dma, dma,
            dma((4,)), dma((4,)),
            dma((3, 2)), dma((2,)), dma((2, 2)),
            dma, dma,
        ],
        compiler_params=pltpu.CompilerParams(
            collective_id=0, has_side_effects=True, vmem_limit_bytes=60 * 1024 * 1024
        ),
        name="head_step",
    )(teacher_features, student_features, prototypes)
    return feature_grad, proto_grad[None]


def solution(mesh):
    return jax.shard_map(
        on_device,
        mesh=mesh,
        in_specs=(P(("rows", "protos"), None), P(("rows", "protos"), None), P("protos", None)),
        out_specs=(P(("rows", "protos"), None), P("rows", "protos", None)),
        check_vma=False,
    )
```

time: 736 us -> 94.9 us (0.13)
  blocking collectives: 371 us -> 0 us
  waiting for transfers between devices: 264 us -> 0 us
  Pallas kernels: 0 us -> 90.6 us
  matrix products: 66.9 us -> 0 us
  other arithmetic: 14.6 us -> 0 us
  between operations: 14.1 us -> 0.64 us
    psum x6 -> x0, blocking collectives: 292 us -> none  [the longest x3 173 us: on_device(): row_whole = lax.psum(row_part, 'protos')]
    reduce_scatter x2 -> x0, waiting for transfers between devices: 264 us -> none  [the longest x1 213 us: on_device(): lax.psum_scatter(feature_term, 'protos', scatter_dimension=0, tiled=True)]
    pallas_call x0 -> x1, Pallas kernels: none -> 90.6 us  [on_device(): pl.pallas_call(functools.partial(kernel, n_rows, n_protos, rows * n_rows)...]
    all_gather x2 -> x0, blocking collectives: 78.3 us -> none  [the longest x1 41.6 us: on_device(): lax.all_gather(local_s, 'protos', axis=0, tiled=True)]
    dot_general x10 -> x0, matrix products: 66.9 us -> none  [the longest x3 28.9 us: on_device(): row_part = jnp.dot(kernel, col_scale, precision=lax.Precision.HIGHEST)]
    convert_element_type x3 -> x0, other arithmetic: 8.9 us -> none  [the longest x1 7.33 us: on_device(): delta = (probs - target).astype(jnp.bfloat16)]
  transfers between devices with their start and end apart: 2 -> 0, of which waited for: 2 -> 0; matrix products, arithmetic and copies ran while one was open for 1% -> 0% of each run, Pallas kernels for 0% -> 0%
where the time goes in v1:
time: 94.9 us; the launch traced here: 94.7 us
  Pallas kernels  90.6 us (95%)
  local copies, waits for them, and re-layouts  3.41 us (4%)
    pallas_call x1, Pallas kernels, on_device(): pl.pallas_call(functools.partial(kernel, n_rows, n_protos, rows * n_rows)...  90.6 us
    unnamed x2, local copies, waits for them, and re-layouts  3.41 us

profile of v1, /device:TPU:1, one launch (start us, length us, event | category | flops | bytes accessed | tf_op | source)
XLA Modules:
  0.0 94.7 jit_solution(9702906963086533325)
XLA Ops:
  0.6 90.6 %head_step.1 = (f32[16,384]{1,0:T(8,128)}, f32[512,384]{1,0:T(8,128)}) custom-call(bf16[16,384]{1,0:T(8,128)(2,1)} %t_ref.1, bf16[16,384]{1,0:T(8,128)(2,1)} %s_ref.1, bf16[4096,384]{1,0:T(8,128)(2,1)} %w_ref.1), custom_call_target="tpu_custom_call" | custom-call | tf_op jit(solution)/shard_map/head_step/pallas_call | solution.py:317
  91.3 1.3 %copy.7 = f32[16,384]{1,0:T(8,128)} copy(f32[16,384]{1,0:T(8,128)} %get-tuple-element.8) | data formatting | bytes 49152
  92.6 2.1 %copy.8 = f32[1,512,384]{2,1,0:T(8,128)} copy(f32[1,512,384]{2,1,0:T(8,128)} %bitcast.1) | data formatting | bytes 1572864

commit v2 on v1

v2 whole, which is shorter than its diff:
```python
import functools
import math

import jax
import jax.numpy as jnp
from jax import lax
from jax.experimental import pallas as pl
from jax.experimental.pallas import tpu as pltpu
from jax.sharding import PartitionSpec as P

K = 131072
PASSES = 3
EPS = 1e-06
LANES = 128
STEP = 256
WIDE = 1024
MIDDLE = 512
CHIPS = 4
LINES = 4
MESH = pl.DeviceIdType.MESH
f32 = jnp.float32
bf16 = jnp.bfloat16


def unitize(values):
    values = values.astype(f32)
    return (values * lax.rsqrt(jnp.sum(values * values, axis=1, keepdims=True) + EPS)).astype(bf16)


def kernel(
    n_rows, n_protos, factor_rows,
    t_ref, s_ref, w_ref, fg_ref, pg_ref,
    tg, sg, uw, km, pm, st, rb, qb, acc, cbuf, cvec, rbuf, qbuf,
    wv, dall, fsend, fline, fout, frecv, psend, precv, xsend, relay, xrecv, hold, own,
    w_sem, t_ss, tz_rs, ty_rs, s_ss, sz_rs, sy_rs, c_ss, c_rs, r_ss, r_rs, q_ss, q_rs,
    p_ss, p_rs, x_ss, l_rs, x_rs, f_ss, fy_rs, g_ss, f_rs,
):
    rows, protos = km.shape
    depth = uw.shape[1]
    block = t_ref.shape[0]
    chunk = protos // n_rows
    half = chunk // 2
    scale = 1.5 * math.sqrt(depth)
    power = scale * math.log2(math.e)
    factor = scale * K / factor_rows
    r = lax.axis_index("rows")
    p = lax.axis_index("protos")

    barrier = pltpu.get_barrier_semaphore()

    depth_z = n_protos // LINES
    y, z = lax.div(p, depth_z), lax.rem(p, depth_z)
    x, core = lax.div(r, 2), lax.rem(r, 2)

    def spot(dy, dz):
        return lax.rem(y + dy, LINES) * depth_z + lax.rem(z + dz, depth_z)

    def far_first(j):
        return depth_z // 2 + lax.div(j + 1, 2) * (1 - 2 * lax.rem(j, 2))

    def remote(source, target, send_sem, recv_sem, to):
        pltpu.make_async_remote_copy(
            src_ref=source, dst_ref=target, send_sem=send_sem, recv_sem=recv_sem,
            device_id=to, device_id_type=MESH,
        ).start()

    def greet(to):
        pl.semaphore_signal(barrier, inc=1, device_id=to, device_id_type=MESH)

    def all_protos(visit):
        def one(j, _):
            for dy in (2, 1, 3, 0):
                visit(spot(dy, far_first(j)))
            return 0

        lax.fori_loop(0, depth_z - 1, one, 0)
        for dy in (2, 1, 3):
            visit(spot(dy, 0))

    def all_rows(visit):
        for ahead in (2, 1, 3):
            for other in range(2):
                visit(lax.rem(x + ahead, CHIPS) * 2 + lax.rem(core + other, 2))
        visit(x * 2 + 1 - core)

    all_protos(lambda q: greet({"protos": q}))
    all_rows(lambda q: greet({"rows": q}))

    def drain(view, sem):
        pltpu.make_async_copy(view, view, sem).wait()

    fetch = pltpu.make_async_copy(w_ref, wv, w_sem)
    fetch.start()
    tg[p] = unitize(t_ref[...])
    sg[p] = unitize(s_ref[...])
    pl.semaphore_wait(barrier, n_protos + n_rows - 2)

    def along_z(buf, send_sem, recv_sem):
        for j in range(depth_z - 1):
            dz = depth_z // 2 + (j + 1) // 2 * (1 - 2 * (j % 2))
            remote(
                buf.at[p], buf.at[p], send_sem, recv_sem.at[dz - 1], {"protos": spot(0, dz)}
            )

    def along_y(buf, q, send_sem, recv_sem, distances):
        for dy in distances:
            to = lax.rem(y + dy, LINES) * depth_z + z
            remote(buf.at[q], buf.at[q], send_sem, recv_sem.at[dy - 1], {"protos": to})

    def pass_on(buf, send_sem, z_sem, y_sem):
        along_y(buf, p, send_sem, y_sem, (1, 3))
        for j in reversed(range(depth_z - 1)):
            dz = depth_z // 2 + (j + 1) // 2 * (1 - 2 * (j % 2))
            q = spot(0, depth_z - dz)
            drain(buf.at[q], z_sem.at[dz - 1])
            along_y(buf, q, send_sem, y_sem, (1, 3))
        for k in range(depth_z):
            along_y(buf, y * depth_z + k, send_sem, y_sem, (2,))

    def column_here(buf, dy, y_sem):
        line = lax.rem(y + LINES - dy, LINES) * depth_z
        drain(buf.at[pl.ds(line, depth_z)], y_sem.at[dy - 1])

    along_z(tg, t_ss, tz_rs)
    along_z(sg, s_ss, sz_rs)
    fetch.wait()

    def unit_step(i, _):
        at = pl.ds(pl.multiple_of(i * STEP, STEP), STEP)
        uw[at, :] = unitize(wv[at, :])
        return 0

    lax.fori_loop(0, protos // STEP, unit_step, 0)

    others = pl.ds(0, n_protos - 1)
    pass_on(tg, t_ss, tz_rs, ty_rs)
    def logits(left, i, width):
        at = pl.ds(pl.multiple_of(i * width, width), width)
        values = lax.dot_general(
            left, uw[at, :], (((1,), (1,)), ((), ())), preferred_element_type=f32
        )
        return at, jnp.exp2(values * power)

    pair_rows = 2 * depth_z * block

    def kernel_half(pair, first):
        lines = pl.ds(pair * 2 * depth_z, 2 * depth_z)
        here = pl.ds(pl.multiple_of(pair * pair_rows, pair_rows), pair_rows)
        teacher = tg[lines].reshape(pair_rows, depth)

        def one(i, _):
            at, values = logits(teacher, i, WIDE)
            km[here, at] = values
            part = jnp.sum(values, axis=0, keepdims=True)
            cbuf[0, r, :, at] = part if first else cbuf[0, r, :, at] + part
            return 0

        lax.fori_loop(0, protos // WIDE, one, 0)

    odd = lax.rem(y, 2)
    near = 3 - 2 * odd
    line = lax.rem(y + LINES - near, LINES) * depth_z
    drain(tg.at[pl.ds(line, depth_z)], ty_rs.at[near - 1])
    kernel_half(lax.div(y, 2), True)
    pass_on(sg, s_ss, sz_rs, sy_rs)
    line = lax.rem(y + near, LINES) * depth_z
    drain(tg.at[pl.ds(line, depth_z)], ty_rs.at[LINES - near - 1])
    column_here(tg, 2, ty_rs)
    kernel_half(1 - lax.div(y, 2), False)

    def column(values):
        return jnp.transpose(jnp.broadcast_to(values, (LANES, LANES)))

    def to_columns(values, ref):
        for g in range(rows // LANES):
            ref[g * LANES:(g + 1) * LANES, :] = column(values[:, g * LANES:(g + 1) * LANES])

    def lane_sums(acc, store):
        for g in range(rows // LANES):
            turned = jnp.transpose(acc[g * LANES:(g + 1) * LANES, :])
            store(slice(g * LANES, (g + 1) * LANES), jnp.sum(turned, axis=0, keepdims=True))

    tiles = protos // LANES

    def lane(j):
        return slice(j * LANES, (j + 1) * LANES)

    def column_pass(step):
        def one(i, sums):
            at = pl.ds(pl.multiple_of(i * 8, 8), 8)
            value = rb[at, :]
            return tuple(sums[j] + km[at, lane(j)] * value for j in range(tiles))

        sums = lax.fori_loop(
            0, rows // 8, one, tuple(jnp.zeros((8, LANES), f32) for _ in range(tiles)), unroll=2
        )
        for j in range(tiles):
            cbuf[step, r, :, lane(j)] = jnp.sum(sums[j], axis=0, keepdims=True)

    def row_pass(step):
        cols = [jnp.broadcast_to(cvec[:, lane(j)], (8, LANES)) for j in range(tiles)]

        def one(i, _):
            at = pl.ds(pl.multiple_of(i * 8, 8), 8)
            parts = [km[at, lane(j)] * cols[j] for j in range(4)]
            for j in range(4, tiles):
                parts[j % 4] = parts[j % 4] + km[at, lane(j)] * cols[j]
            acc[at, :] = (parts[0] + parts[1]) + (parts[2] + parts[3])
            return 0

        lax.fori_loop(0, rows // 8, one, 0, unroll=2)

        def store(at, value):
            rbuf[step, p, :, at] = value

        lane_sums(acc, store)

    steps = protos // MIDDLE

    def student(begin, end):
        units = sg[...].reshape(rows, depth)

        def one(i, _):
            at, values = logits(units, i, MIDDLE)
            pm[:, at] = values
            qb[...] += sum(values[:, j * LANES:(j + 1) * LANES] for j in range(MIDDLE // LANES))
            return 0

        lax.fori_loop(begin, end, one, 0)

    def student_begin():
        for dy in (1, 2, 3):
            column_here(sg, dy, sy_rs)
        qb[...] = jnp.zeros_like(qb)
        student(0, steps // 2)

    def student_end():
        student(steps // 2, steps)

        def store(at, value):
            qbuf[p, :, at] = value

        lane_sums(qb, store)
        all_protos(lambda q: remote(qbuf.at[p], qbuf.at[p], q_ss, q_rs, {"protos": q}))

    for step in range(PASSES):
        if step > 0:
            column_pass(step)
        mine = cbuf.at[step, r]
        all_rows(lambda q: remote(mine, mine, c_ss.at[step], c_rs.at[step], {"rows": q}))
        if step == 1:
            student_end()
        elif step == 2:
            drain(qbuf.at[others], q_rs)
            to_columns(1.0 / jnp.sum(qbuf[...], axis=0), qb)
        drain(cbuf.at[step, pl.ds(0, n_rows - 1)], c_rs.at[step])
        cvec[...] = 1.0 / jnp.sum(cbuf[step], axis=0)
        row_pass(step)
        mine = rbuf.at[step, p]
        all_protos(lambda q: remote(mine, mine, r_ss.at[step], r_rs.at[step], {"protos": q}))
        if step == 0:
            student_begin()
        elif step == 1:
            st[...] = jnp.transpose(sg[...].reshape(rows, depth).astype(f32)).astype(bf16)
        drain(rbuf.at[step, others], r_rs.at[step])
        to_columns(1.0 / jnp.sum(rbuf[step], axis=0), rb)

    def delta(owner):
        at = pl.ds(pl.multiple_of(owner * chunk, chunk), chunk)
        cols = cvec[:, at]

        def one(i, _):
            here = pl.ds(pl.multiple_of(i * 16, 16), 16)
            row = jnp.concatenate([rb[here, :]] * (chunk // LANES), axis=1)
            inv = jnp.concatenate([qb[here, :]] * (chunk // LANES), axis=1)
            value = pm[here, at] * inv - km[here, at] * row * cols
            dall[here, at] = value.astype(bf16)
            return 0

        lax.fori_loop(0, rows // 16, one, 0, unroll=2)

    def term(owner):
        at = pl.ds(pl.multiple_of(owner * chunk, chunk), chunk)
        return jnp.dot(st[...], dall[:, at], preferred_element_type=f32)

    def features():
        half_rows = rows // 2

        def one(i, _):
            here = pl.ds(pl.multiple_of(i * half_rows, half_rows), half_rows)
            part = jnp.dot(dall[here, :], uw[...], preferred_element_type=f32).astype(bf16)
            to = pl.ds(i * (n_protos // 2), n_protos // 2)
            fsend[to] = part.reshape(n_protos // 2, block, depth)
            return 0

        lax.fori_loop(0, 2, one, 0)

        def post(j, _):
            dz = far_first(j)
            for dy in (2, 1, 3):
                q = spot(dy, dz)
                to = lax.rem(y + dy, LINES) * depth_z + z
                remote(fsend.at[q], fline.at[j, dy - 1], f_ss, fy_rs.at[j], {"protos": to})
            return 0

        lax.fori_loop(0, depth_z, post, 0)

    def features_on():
        def one(j, _):
            q = spot(0, far_first(j))
            drain(fline.at[j], fy_rs.at[j])
            value = fsend[q].astype(f32) + fline[j, 0].astype(f32)
            value = value + (fline[j, 1].astype(f32) + fline[j, 2].astype(f32))
            fout[j] = value.astype(bf16)
            return 0

        def step(j, _):
            one(j, 0)
            q = spot(0, far_first(j))
            remote(fout.at[j], frecv.at[z], g_ss, f_rs, {"protos": q})
            return 0

        lax.fori_loop(0, depth_z - 1, step, 0)
        one(depth_z - 1, 0)
        frecv[z] = fout[depth_z - 1]

    def send(source, target, send_sem, recv_sem, to):
        remote(source, target, send_sem, recv_sem, {"rows": to})

    up = lax.rem(x + 1, CHIPS) * 2 + core
    down = lax.rem(x + CHIPS - 1, CHIPS) * 2 + core
    mate = x * 2 + 1 - core

    chips = [lax.rem(x + ahead, CHIPS) for ahead in (2, 1, 3, 0)]

    def to_mate(k):
        part = term(chips[k] * 2 + 1 - core)
        psend[k, 0] = part[:, :half].astype(bf16)
        psend[k, 1] = part[:, half:].astype(bf16)
        send(psend.at[k], precv.at[k], p_ss.at[k], p_rs.at[k], mate)

    def with_mate(k):
        part = term(chips[k] * 2 + core)
        drain(precv.at[k], p_rs.at[k])
        return part[:, :half] + precv[k, 0].astype(f32), part[:, half:] + precv[k, 1].astype(f32)

    delta(chips[0] * 2 + 1 - core)
    to_mate(0)
    delta(chips[0] * 2 + core)
    low, high = with_mate(0)
    xsend[0, 0] = low.astype(bf16)
    xsend[0, 1] = high.astype(bf16)
    send(xsend.at[0, 0], relay.at[0], x_ss.at[0, 0], l_rs.at[0], up)
    send(xsend.at[0, 1], relay.at[1], x_ss.at[0, 1], l_rs.at[1], down)
    def deltas(k):
        delta(chips[k] * 2 + 1 - core)
        delta(chips[k] * 2 + core)

    deltas(1)
    to_mate(1)
    deltas(2)
    to_mate(2)
    low, high = with_mate(1)
    hold[0] = low
    xsend[1, 1] = high.astype(bf16)
    send(xsend.at[1, 1], xrecv.at[0, 1], x_ss.at[1, 1], x_rs.at[0, 1], up)
    low, high = with_mate(2)
    hold[1] = high
    xsend[2, 0] = low.astype(bf16)
    send(xsend.at[2, 0], xrecv.at[1, 0], x_ss.at[2, 0], x_rs.at[1, 0], down)
    deltas(3)
    features()
    to_mate(3)
    low, high = with_mate(3)
    own[0] = low
    own[1] = high

    drain(relay.at[0], l_rs.at[0])
    xsend[1, 0] = (hold[0] + relay[0].astype(f32)).astype(bf16)
    send(xsend.at[1, 0], xrecv.at[0, 0], x_ss.at[1, 0], x_rs.at[0, 0], up)
    drain(relay.at[1], l_rs.at[1])
    xsend[2, 1] = (hold[1] + relay[1].astype(f32)).astype(bf16)
    send(xsend.at[2, 1], xrecv.at[1, 1], x_ss.at[2, 1], x_rs.at[1, 1], down)

    features_on()
    drain(frecv.at[pl.ds(0, depth_z - 1)], f_rs)
    total = jnp.zeros((block, depth), f32)
    total = lax.fori_loop(0, depth_z, lambda i, a: a + frecv[i].astype(f32), total)
    fg_ref[...] = scale * total

    for side in range(2):
        for h in range(2):
            drain(xrecv.at[side, h], x_rs.at[side, h])
    for h in range(2):
        whole = own[h] + xrecv[0, h].astype(f32) + xrecv[1, h].astype(f32)
        pg_ref[h * half:(h + 1) * half, :] = jnp.transpose(factor * whole)

    drain(tg.at[others], t_ss)
    drain(sg.at[others], s_ss)
    drain(qbuf.at[others], q_ss)
    drain(fline, f_ss)
    drain(frecv.at[pl.ds(0, depth_z - 1)], g_ss)
    for step in range(PASSES):
        drain(cbuf.at[step, pl.ds(0, n_rows - 1)], c_ss.at[step])
        drain(rbuf.at[step, others], r_ss.at[step])
    for k in range(4):
        drain(psend.at[k], p_ss.at[k])
    for k in range(3):
        for h in range(2):
            drain(xsend.at[k, h], x_ss.at[k, h])


def on_device(teacher_features, student_features, prototypes):
    n_rows, n_protos = lax.axis_size("rows"), lax.axis_size("protos")
    block, depth = teacher_features.shape
    protos = prototypes.shape[0]
    rows = block * n_protos
    chunk = protos // n_rows
    half = chunk // 2
    depth_z = n_protos // LINES
    dma = pltpu.SemaphoreType.DMA
    vmem = pltpu.VMEM
    feature_grad, proto_grad = pl.pallas_call(
        functools.partial(kernel, n_rows, n_protos, rows * n_rows),
        out_shape=(
            jax.ShapeDtypeStruct((block, depth), f32),
            jax.ShapeDtypeStruct((chunk, depth), f32),
        ),
        in_specs=[pl.BlockSpec(memory_space=pltpu.VMEM)] * 2 + [pl.BlockSpec(memory_space=pl.ANY)],
        out_specs=(pl.BlockSpec(memory_space=pltpu.VMEM),) * 2,
        scratch_shapes=[
            vmem((n_protos, block, depth), bf16),
            vmem((n_protos, block, depth), bf16),
            vmem((protos, depth), bf16),
            vmem((rows, protos), f32),
            vmem((rows, protos), f32),
            vmem((depth, rows), bf16),
            vmem((rows, LANES), f32),
            vmem((rows, LANES), f32),
            vmem((rows, LANES), f32),
            vmem((PASSES, n_rows, 1, protos), f32),
            vmem((1, protos), f32),
            vmem((PASSES, n_protos, 1, rows), f32),
            vmem((n_protos, 1, rows), f32),
            vmem((protos, depth), bf16),
            vmem((rows, protos), bf16),
            vmem((n_protos, block, depth), bf16),
            vmem((depth_z, LINES - 1, block, depth), bf16),
            vmem((depth_z, block, depth), bf16),
            vmem((depth_z, block, depth), bf16),
            vmem((4, 2, depth, half), bf16),
            vmem((4, 2, depth, half), bf16),
            vmem((3, 2, depth, half), bf16),
            vmem((2, depth, half), bf16),
            vmem((2, 2, depth, half), bf16),
            vmem((2, depth, half), f32),
            vmem((2, depth, half), f32),
            dma, dma, dma((depth_z - 1,)), dma((LINES - 1,)),
            dma, dma((depth_z - 1,)), dma((LINES - 1,)),
            dma((PASSES,)), dma((PASSES,)), dma((PASSES,)), dma((PASSES,)),
            dma, dma,
            dma((4,)), dma((4,)),
            dma((3, 2)), dma((2,)), dma((2, 2)),
            dma, dma((depth_z,)), dma, dma,
        ],
        compiler_params=pltpu.CompilerParams(
            collective_id=0, has_side_effects=True, vmem_limit_bytes=60 * 1024 * 1024
        ),
        name="head_step",
    )(teacher_features, student_features, prototypes)
    return feature_grad, proto_grad[None]


def solution(mesh):
    return jax.shard_map(
        on_device,
        mesh=mesh,
        in_specs=(P(("rows", "protos"), None), P(("rows", "protos"), None), P("protos", None)),
        out_specs=(P(("rows", "protos"), None), P("rows", "protos", None)),
        check_vma=False,
    )
```

time: 94.9 us -> 82.6 us (0.87)
  Pallas kernels: 90.6 us -> 78.3 us
    pallas_call x1, Pallas kernels: 90.6 us -> 78.3 us  [on_device(): pl.pallas_call(functools.partial(kernel, n_rows, n_protos, rows * n_rows)...]
where the time goes in v2:
time: 82.6 us; the launch traced here: 82.3 us
  Pallas kernels  78.3 us (95%)
  local copies, waits for them, and re-layouts  3.41 us (4%)
    pallas_call x1, Pallas kernels, on_device(): pl.pallas_call(functools.partial(kernel, n_rows, n_protos, rows * n_rows)...  78.3 us
    unnamed x2, local copies, waits for them, and re-layouts  3.41 us

profile of v2, /device:TPU:1, one launch (start us, length us, event | category | flops | bytes accessed | tf_op | source)
XLA Modules:
  0.0 82.3 jit_solution(9246516812430977924)
XLA Ops:
  0.6 78.3 %head_step.1 = (f32[16,384]{1,0:T(8,128)}, f32[512,384]{1,0:T(8,128)}) custom-call(bf16[16,384]{1,0:T(8,128)(2,1)} %t_ref.1, bf16[16,384]{1,0:T(8,128)(2,1)} %s_ref.1, bf16[4096,384]{1,0:T(8,128)(2,1)} %w_ref.1), custom_call_target="tpu_custom_call" | custom-call | tf_op jit(solution)/shard_map/head_step/pallas_call | solution.py:423
  78.9 1.3 %copy.7 = f32[16,384]{1,0:T(8,128)} copy(f32[16,384]{1,0:T(8,128)} %get-tuple-element.8) | data formatting | bytes 49152
  80.2 2.1 %copy.8 = f32[1,512,384]{2,1,0:T(8,128)} copy(f32[1,512,384]{2,1,0:T(8,128)} %bitcast.1) | data formatting | bytes 1572864

commit v3 on v2

--- a/solution.py
+++ b/solution.py
@@ -29,10 +29,10 @@
 
 def kernel(
     n_rows, n_protos, factor_rows,
-    t_ref, s_ref, w_ref, fg_ref, pg_ref,
-    tg, sg, uw, km, pm, st, rb, qb, acc, cbuf, cvec, rbuf, qbuf,
-    wv, dall, fsend, fline, fout, frecv, psend, precv, xsend, relay, xrecv, hold, own,
-    w_sem, t_ss, tz_rs, ty_rs, s_ss, sz_rs, sy_rs, c_ss, c_rs, r_ss, r_rs, q_ss, q_rs,
+    t_hbm, s_hbm, w_ref, fg_ref, pg_ref,
+    tg, sg, uw, km, pm, st, rb, qb, acc, cacc, cbuf, cvec, rbuf, qbuf,
+    wv, t_ref, s_ref, dall, fsend, fline, fout, frecv, psend, precv, xsend, relay, xrecv, hold, own,
+    in_sem, t_ss, tz_rs, ty_rs, s_ss, sz_rs, sy_rs, c_ss, c_rs, r_ss, r_rs, q_ss, q_rs,
     p_ss, p_rs, x_ss, l_rs, x_rs, f_ss, fy_rs, g_ss, f_rs,
 ):
     rows, protos = km.shape
@@ -46,6 +46,13 @@
     r = lax.axis_index("rows")
     p = lax.axis_index("protos")
 
+    loads = [
+        pltpu.make_async_copy(source, target, in_sem.at[k])
+        for k, (source, target) in enumerate(((t_hbm, t_ref), (s_hbm, s_ref), (w_ref, wv)))
+    ]
+    for copy in loads:
+        copy.start()
+
     barrier = pltpu.get_barrier_semaphore()
 
     depth_z = n_protos // LINES
@@ -89,8 +96,8 @@
     def drain(view, sem):
         pltpu.make_async_copy(view, view, sem).wait()
 
-    fetch = pltpu.make_async_copy(w_ref, wv, w_sem)
-    fetch.start()
+    for copy in loads[:2]:
+        copy.wait()
     tg[p] = unitize(t_ref[...])
     sg[p] = unitize(s_ref[...])
     pl.semaphore_wait(barrier, n_protos + n_rows - 2)
@@ -123,7 +130,7 @@
 
     along_z(tg, t_ss, tz_rs)
     along_z(sg, s_ss, sz_rs)
-    fetch.wait()
+    loads[2].wait()
 
     def unit_step(i, _):
         at = pl.ds(pl.multiple_of(i * STEP, STEP), STEP)
@@ -143,30 +150,32 @@
 
     pair_rows = 2 * depth_z * block
 
-    def kernel_half(pair, first):
+    def kernel_half(pair, c, first):
         lines = pl.ds(pair * 2 * depth_z, 2 * depth_z)
         here = pl.ds(pl.multiple_of(pair * pair_rows, pair_rows), pair_rows)
         teacher = tg[lines].reshape(pair_rows, depth)
+        steps = protos // 2 // WIDE
 
         def one(i, _):
-            at, values = logits(teacher, i, WIDE)
+            at, values = logits(teacher, c * steps + i, WIDE)
             km[here, at] = values
             part = jnp.sum(values, axis=0, keepdims=True)
-            cbuf[0, r, :, at] = part if first else cbuf[0, r, :, at] + part
-            return 0
-
-        lax.fori_loop(0, protos // WIDE, one, 0)
+            to = pl.ds(pl.multiple_of(i * WIDE, WIDE), WIDE)
+            cbuf[0, c, r, :, to] = part if first else cbuf[0, c, r, :, to] + part
+            return 0
+
+        lax.fori_loop(0, steps, one, 0)
 
     odd = lax.rem(y, 2)
     near = 3 - 2 * odd
     line = lax.rem(y + LINES - near, LINES) * depth_z
     drain(tg.at[pl.ds(line, depth_z)], ty_rs.at[near - 1])
-    kernel_half(lax.div(y, 2), True)
+    kernel_half(lax.div(y, 2), 0, True)
+    kernel_half(lax.div(y, 2), 1, True)
     pass_on(sg, s_ss, sz_rs, sy_rs)
     line = lax.rem(y + near, LINES) * depth_z
     drain(tg.at[pl.ds(line, depth_z)], ty_rs.at[LINES - near - 1])
     column_here(tg, 2, ty_rs)
-    kernel_half(1 - lax.div(y, 2), False)
 
     def column(values):
         return jnp.transpose(jnp.broadcast_to(values, (LANES, LANES)))
@@ -175,45 +184,95 @@
         for g in range(rows // LANES):
             ref[g * LANES:(g + 1) * LANES, :] = column(values[:, g * LANES:(g + 1) * LANES])
 
-    def lane_sums(acc, store):
-        for g in range(rows // LANES):
+    def lane_sums(acc, store, groups):
+        for g in groups:
             turned = jnp.transpose(acc[g * LANES:(g + 1) * LANES, :])
-            store(slice(g * LANES, (g + 1) * LANES), jnp.sum(turned, axis=0, keepdims=True))
+            at = slice((g - groups[0]) * LANES, (g - groups[0] + 1) * LANES)
+            store(at, jnp.sum(turned, axis=0, keepdims=True))
 
     tiles = protos // LANES
+    groups = rows // LANES
+    side = protos // 2
+    wing = rows // 2
 
     def lane(j):
         return slice(j * LANES, (j + 1) * LANES)
 
+    def rows_of(i):
+        return pl.ds(pl.multiple_of(i * 8, 8), 8)
+
+    def column_sweep(h, which):
+        def one(i, sums):
+            at = rows_of(i)
+            value = rb[at, :]
+            return tuple(s + km[at, lane(j)] * value for s, j in zip(sums, which))
+
+        return lax.fori_loop(
+            h * wing // 8, (h + 1) * wing // 8, one,
+            tuple(jnp.zeros((8, LANES), f32) for _ in which), unroll=2,
+        )
+
+    def row_sweep(h, c):
+        which = range(c * tiles // 2, (c + 1) * tiles // 2)
+        cols = [jnp.broadcast_to(cvec[:, lane(j)], (8, LANES)) for j in which]
+
+        def one(i, _):
+            at = rows_of(i)
+            parts = [km[at, lane(j)] * col for j, col in zip(which[:4], cols[:4])]
+            for k in range(4, len(which)):
+                parts[k % 4] = parts[k % 4] + km[at, lane(which[k])] * cols[k]
+            total = (parts[0] + parts[1]) + (parts[2] + parts[3])
+            acc[at, :] = total if c == 0 else acc[at, :] + total
+            return 0
+
+        lax.fori_loop(h * wing // 8, (h + 1) * wing // 8, one, 0, unroll=2)
+
+    def send_columns(step, c):
+        mine = cbuf.at[step, c, r]
+        sems = c_ss.at[step, c], c_rs.at[step, c]
+        all_rows(lambda q: remote(mine, mine, *sems, {"rows": q}))
+
+    def send_sums(step, h):
+        mine = rbuf.at[step, h, p]
+        sems = r_ss.at[step, h], r_rs.at[step, h]
+        all_protos(lambda q: remote(mine, mine, *sems, {"protos": q}))
+
+    def take_columns(step, c):
+        drain(cbuf.at[step, c, pl.ds(0, n_rows - 1)], c_rs.at[step, c])
+        cvec[:, c * side:(c + 1) * side] = 1.0 / jnp.sum(cbuf[step, c], axis=0)
+
+    def take_sums(step, h):
+        drain(rbuf.at[step, h, others], r_rs.at[step, h])
+        values = 1.0 / jnp.sum(rbuf[step, h], axis=0)
+        for g in range(groups // 2):
+            at = h * wing + g * LANES
+            rb[at:at + LANES, :] = column(values[:, lane(g)])
+
     def column_pass(step):
-        def one(i, sums):
-            at = pl.ds(pl.multiple_of(i * 8, 8), 8)
-            value = rb[at, :]
-            return tuple(sums[j] + km[at, lane(j)] * value for j in range(tiles))
-
-        sums = lax.fori_loop(
-            0, rows // 8, one, tuple(jnp.zeros((8, LANES), f32) for _ in range(tiles)), unroll=2
-        )
-        for j in range(tiles):
-            cbuf[step, r, :, lane(j)] = jnp.sum(sums[j], axis=0, keepdims=True)
+        take_sums(step - 1, 0)
+        for j, value in enumerate(column_sweep(0, range(tiles))):
+            cacc[:, lane(j)] = value
+        take_sums(step - 1, 1)
+        for c in range(2):
+            which = range(c * tiles // 2, (c + 1) * tiles // 2)
+            for j, value in zip(which, column_sweep(1, which)):
+                value = jnp.sum(value + cacc[:, lane(j)], axis=0, keepdims=True)
+                cbuf[step, c, r, :, lane(j - which[0])] = value
+            send_columns(step, c)
 
     def row_pass(step):
-        cols = [jnp.broadcast_to(cvec[:, lane(j)], (8, LANES)) for j in range(tiles)]
-
-        def one(i, _):
-            at = pl.ds(pl.multiple_of(i * 8, 8), 8)
-            parts = [km[at, lane(j)] * cols[j] for j in range(4)]
-            for j in range(4, tiles):
-                parts[j % 4] = parts[j % 4] + km[at, lane(j)] * cols[j]
-            acc[at, :] = (parts[0] + parts[1]) + (parts[2] + parts[3])
-            return 0
-
-        lax.fori_loop(0, rows // 8, one, 0, unroll=2)
-
-        def store(at, value):
-            rbuf[step, p, :, at] = value
-
-        lane_sums(acc, store)
+        take_columns(step, 0)
+        row_sweep(0, 0)
+        row_sweep(1, 0)
+        take_columns(step, 1)
+        for h in range(2):
+            row_sweep(h, 1)
+
+            def store(at, value):
+                rbuf[step, h, p, :, at] = value
+
+            lane_sums(acc, store, range(h * groups // 2, (h + 1) * groups // 2))
+            send_sums(step, h)
 
     steps = protos // MIDDLE
 
@@ -240,30 +299,28 @@
         def store(at, value):
             qbuf[p, :, at] = value
 
-        lane_sums(qb, store)
+        lane_sums(qb, store, range(groups))
         all_protos(lambda q: remote(qbuf.at[p], qbuf.at[p], q_ss, q_rs, {"protos": q}))
+
+    for c in range(2):
+        kernel_half(1 - lax.div(y, 2), c, False)
+        send_columns(0, c)
 
     for step in range(PASSES):
         if step > 0:
             column_pass(step)
-        mine = cbuf.at[step, r]
-        all_rows(lambda q: remote(mine, mine, c_ss.at[step], c_rs.at[step], {"rows": q}))
         if step == 1:
             student_end()
         elif step == 2:
             drain(qbuf.at[others], q_rs)
             to_columns(1.0 / jnp.sum(qbuf[...], axis=0), qb)
-        drain(cbuf.at[step, pl.ds(0, n_rows - 1)], c_rs.at[step])
-        cvec[...] = 1.0 / jnp.sum(cbuf[step], axis=0)
         row_pass(step)
-        mine = rbuf.at[step, p]
-        all_protos(lambda q: remote(mine, mine, r_ss.at[step], r_rs.at[step], {"protos": q}))
         if step == 0:
             student_begin()
         elif step == 1:
             st[...] = jnp.transpose(sg[...].reshape(rows, depth).astype(f32)).astype(bf16)
-        drain(rbuf.at[step, others], r_rs.at[step])
-        to_columns(1.0 / jnp.sum(rbuf[step], axis=0), rb)
+    for h in range(2):
+        take_sums(PASSES - 1, h)
 
     def delta(owner):
         at = pl.ds(pl.multiple_of(owner * chunk, chunk), chunk)
@@ -401,13 +458,25 @@
     drain(fline, f_ss)
     drain(frecv.at[pl.ds(0, depth_z - 1)], g_ss)
     for step in range(PASSES):
-        drain(cbuf.at[step, pl.ds(0, n_rows - 1)], c_ss.at[step])
-        drain(rbuf.at[step, others], r_ss.at[step])
+        for h in range(2):
+            drain(cbuf.at[step, h, pl.ds(0, n_rows - 1)], c_ss.at[step, h])
+            drain(rbuf.at[step, h, others], r_ss.at[step, h])
     for k in range(4):
         drain(psend.at[k], p_ss.at[k])
     for k in range(3):
         for h in range(2):
             drain(xsend.at[k, h], x_ss.at[k, h])
+
+
+def store(feature, proto, feature_out, proto_out, f_sem, p_sem):
+    copies = [
+        pltpu.make_async_copy(proto, proto_out, p_sem),
+        pltpu.make_async_copy(feature, feature_out, f_sem),
+    ]
+    for copy in copies:
+        copy.start()
+    for copy in copies:
+        copy.wait()
 
 
 def on_device(teacher_features, student_features, prototypes):
@@ -426,7 +495,7 @@
             jax.ShapeDtypeStruct((block, depth), f32),
             jax.ShapeDtypeStruct((chunk, depth), f32),
         ),
-        in_specs=[pl.BlockSpec(memory_space=pltpu.VMEM)] * 2 + [pl.BlockSpec(memory_space=pl.ANY)],
+        in_specs=[pl.BlockSpec(memory_space=pltpu.HBM)] * 3,
         out_specs=(pl.BlockSpec(memory_space=pltpu.VMEM),) * 2,
         scratch_shapes=[
             vmem((n_protos, block, depth), bf16),
@@ -438,11 +507,14 @@
             vmem((rows, LANES), f32),
             vmem((rows, LANES), f32),
             vmem((rows, LANES), f32),
-            vmem((PASSES, n_rows, 1, protos), f32),
+            vmem((8, protos), f32),
+            vmem((PASSES, 2, n_rows, 1, protos // 2), f32),
             vmem((1, protos), f32),
-            vmem((PASSES, n_protos, 1, rows), f32),
+            vmem((PASSES, 2, n_protos, 1, rows // 2), f32),
             vmem((n_protos, 1, rows), f32),
             vmem((protos, depth), bf16),
+            vmem((block, depth), bf16),
+            vmem((block, depth), bf16),
             vmem((rows, protos), bf16),
             vmem((n_protos, block, depth), bf16),
             vmem((depth_z, LINES - 1, block, depth), bf16),
@@ -455,19 +527,31 @@
             vmem((2, 2, depth, half), bf16),
             vmem((2, depth, half), f32),
             vmem((2, depth, half), f32),
-            dma, dma, dma((depth_z - 1,)), dma((LINES - 1,)),
+            dma((3,)), dma, dma((depth_z - 1,)), dma((LINES - 1,)),
             dma, dma((depth_z - 1,)), dma((LINES - 1,)),
-            dma((PASSES,)), dma((PASSES,)), dma((PASSES,)), dma((PASSES,)),
+            dma((PASSES, 2)), dma((PASSES, 2)), dma((PASSES, 2)), dma((PASSES, 2)),
             dma, dma,
             dma((4,)), dma((4,)),
             dma((3, 2)), dma((2,)), dma((2, 2)),
             dma, dma((depth_z,)), dma, dma,
         ],
         compiler_params=pltpu.CompilerParams(
-            collective_id=0, has_side_effects=True, vmem_limit_bytes=60 * 1024 * 1024
+            collective_id=0, has_side_effects=True, vmem_limit_bytes=42 * 1024 * 1024
         ),
         name="head_step",
-    )(teacher_features, student_features, prototypes)
+    )(*(pltpu.with_memory_space_constraint(v, pltpu.HBM) for v in (teacher_features, student_features, prototypes)))
+    feature_grad, proto_grad = pl.pallas_call(
+        store,
+        out_shape=(
+            jax.ShapeDtypeStruct((block, depth), f32),
+            jax.ShapeDtypeStruct((chunk, depth), f32),
+        ),
+        in_specs=[pl.BlockSpec(memory_space=pltpu.VMEM)] * 2,
+        out_specs=(pl.BlockSpec(memory_space=pl.ANY),) * 2,
+        scratch_shapes=[dma, dma],
+        compiler_params=pltpu.CompilerParams(vmem_limit_bytes=4 * 1024 * 1024),
+        name="store",
+    )(feature_grad, proto_grad)
     return feature_grad, proto_grad[None]
 
 

time: 82.6 us -> 77.9 us (0.943)
  local copies, waits for them, and re-layouts: 3.41 us -> 0 us
  Pallas kernels: 78.3 us -> 77.1 us
    unnamed x2 -> x0, local copies, waits for them, and re-layouts: 3.41 us -> none
    pallas_call x1, Pallas kernels: 78.3 us -> 76.2 us  [on_device(): pl.pallas_call(functools.partial(kernel, n_rows, n_protos, rows * n_rows)...]
    pallas_call x0 -> x1, Pallas kernels: none -> 0.9 us  [on_device(): pl.pallas_call(store, out_shape=(jax.ShapeDtypeStruct((block, depth), f32...]
where the time goes in v3:
time: 77.9 us; the launch traced here: 77.7 us
  Pallas kernels  77.1 us (99%)
    pallas_call x1, Pallas kernels, on_device(): pl.pallas_call(functools.partial(kernel, n_rows, n_protos, rows * n_rows)...  76.2 us

profile of v3, /device:TPU:1, one launch (start us, length us, event | category | flops | bytes accessed | tf_op | source)
XLA Modules:
  0.0 77.7 jit_solution(11152973892200246918)
XLA Ops:
  0.6 76.2 %head_step.1 = (f32[16,384]{1,0:T(8,128)S(1)}, f32[512,384]{1,0:T(8,128)S(1)}) custom-call(bf16[16,384]{1,0:T(8,128)(2,1)} %t_hbm.1, bf16[16,384]{1,0:T(8,128)(2,1)} %s_hbm.1, bf16[4096,384]{1,0:T(8,128)(2,1)} %w_ref.1), custom_call_target="tpu_custom_call" | custom-call | tf_op jit(solution)/shard_map/head_step/pallas_call | solution.py:492
  76.8 0.9 %store.1 = (f32[16,384]{1,0:T(8,128)}, f32[512,384]{1,0:T(8,128)}) custom-call(f32[16,384]{1,0:T(8,128)S(1)} %get-tuple-element.6.feature, f32[512,384]{1,0:T(8,128)S(1)} %get-tuple-element.7.proto), custom_call_target="tpu_custom_call" | custom-call | tf_op jit(solution)/shard_map/store/pallas_call | solution.py:543

commit v4 on v3

--- a/solution.py
+++ b/solution.py
@@ -30,9 +30,9 @@
 def kernel(
     n_rows, n_protos, factor_rows,
     t_hbm, s_hbm, w_ref, fg_ref, pg_ref,
-    tg, sg, uw, km, pm, st, rb, qb, acc, cacc, cbuf, cvec, rbuf, qbuf,
-    wv, t_ref, s_ref, dall, fsend, fline, fout, frecv, psend, precv, xsend, relay, xrecv, hold, own,
-    in_sem, t_ss, tz_rs, ty_rs, s_ss, sz_rs, sy_rs, c_ss, c_rs, r_ss, r_rs, q_ss, q_rs,
+    tg, sg, uw, km, pm, st, rb, qb, acc, cbuf, cvec, rbuf, qbuf,
+    wv, t_ref, s_ref, dall, fsend, fline, fout, frecv, psend, precv, xsend, relay, xrecv, pown,
+    in_sem, turn_sem, t_ss, tz_rs, ty_rs, s_ss, sz_rs, sy_rs, c_ss, c_rs, r_ss, r_rs, q_ss, q_rs,
     p_ss, p_rs, x_ss, l_rs, x_rs, f_ss, fy_rs, g_ss, f_rs,
 ):
     rows, protos = km.shape
@@ -50,9 +50,6 @@
         pltpu.make_async_copy(source, target, in_sem.at[k])
         for k, (source, target) in enumerate(((t_hbm, t_ref), (s_hbm, s_ref), (w_ref, wv)))
     ]
-    for copy in loads:
-        copy.start()
-
     barrier = pltpu.get_barrier_semaphore()
 
     depth_z = n_protos // LINES
@@ -90,8 +87,13 @@
                 visit(lax.rem(x + ahead, CHIPS) * 2 + lax.rem(core + other, 2))
         visit(x * 2 + 1 - core)
 
-    all_protos(lambda q: greet({"protos": q}))
+    for dz in range(1, depth_z):
+        greet({"protos": spot(0, dz)})
+    for dy in range(1, LINES):
+        greet({"protos": lax.rem(y + dy, LINES) * depth_z + z})
     all_rows(lambda q: greet({"rows": q}))
+    for copy in loads:
+        copy.start()
 
     def drain(view, sem):
         pltpu.make_async_copy(view, view, sem).wait()
@@ -100,7 +102,7 @@
         copy.wait()
     tg[p] = unitize(t_ref[...])
     sg[p] = unitize(s_ref[...])
-    pl.semaphore_wait(barrier, n_protos + n_rows - 2)
+    pl.semaphore_wait(barrier, depth_z + LINES + n_rows - 3)
 
     def along_z(buf, send_sem, recv_sem):
         for j in range(depth_z - 1):
@@ -193,7 +195,6 @@
     tiles = protos // LANES
     groups = rows // LANES
     side = protos // 2
-    wing = rows // 2
 
     def lane(j):
         return slice(j * LANES, (j + 1) * LANES)
@@ -201,18 +202,17 @@
     def rows_of(i):
         return pl.ds(pl.multiple_of(i * 8, 8), 8)
 
-    def column_sweep(h, which):
+    def column_sweep(which):
         def one(i, sums):
             at = rows_of(i)
             value = rb[at, :]
             return tuple(s + km[at, lane(j)] * value for s, j in zip(sums, which))
 
         return lax.fori_loop(
-            h * wing // 8, (h + 1) * wing // 8, one,
-            tuple(jnp.zeros((8, LANES), f32) for _ in which), unroll=2,
+            0, rows // 8, one, tuple(jnp.zeros((8, LANES), f32) for _ in which), unroll=4
         )
 
-    def row_sweep(h, c):
+    def row_sweep(c):
         which = range(c * tiles // 2, (c + 1) * tiles // 2)
         cols = [jnp.broadcast_to(cvec[:, lane(j)], (8, LANES)) for j in which]
 
@@ -225,54 +225,45 @@
             acc[at, :] = total if c == 0 else acc[at, :] + total
             return 0
 
-        lax.fori_loop(h * wing // 8, (h + 1) * wing // 8, one, 0, unroll=2)
+        lax.fori_loop(0, rows // 8, one, 0, unroll=4)
 
     def send_columns(step, c):
         mine = cbuf.at[step, c, r]
         sems = c_ss.at[step, c], c_rs.at[step, c]
         all_rows(lambda q: remote(mine, mine, *sems, {"rows": q}))
 
-    def send_sums(step, h):
-        mine = rbuf.at[step, h, p]
-        sems = r_ss.at[step, h], r_rs.at[step, h]
+    def send_sums(step):
+        mine = rbuf.at[step, p]
+        sems = r_ss.at[step], r_rs.at[step]
         all_protos(lambda q: remote(mine, mine, *sems, {"protos": q}))
 
     def take_columns(step, c):
         drain(cbuf.at[step, c, pl.ds(0, n_rows - 1)], c_rs.at[step, c])
         cvec[:, c * side:(c + 1) * side] = 1.0 / jnp.sum(cbuf[step, c], axis=0)
 
-    def take_sums(step, h):
-        drain(rbuf.at[step, h, others], r_rs.at[step, h])
-        values = 1.0 / jnp.sum(rbuf[step, h], axis=0)
-        for g in range(groups // 2):
-            at = h * wing + g * LANES
-            rb[at:at + LANES, :] = column(values[:, lane(g)])
+    def take_sums(step):
+        drain(rbuf.at[step, others], r_rs.at[step])
+        to_columns(1.0 / jnp.sum(rbuf[step], axis=0), rb)
 
     def column_pass(step):
-        take_sums(step - 1, 0)
-        for j, value in enumerate(column_sweep(0, range(tiles))):
-            cacc[:, lane(j)] = value
-        take_sums(step - 1, 1)
+        take_sums(step - 1)
         for c in range(2):
             which = range(c * tiles // 2, (c + 1) * tiles // 2)
-            for j, value in zip(which, column_sweep(1, which)):
-                value = jnp.sum(value + cacc[:, lane(j)], axis=0, keepdims=True)
+            for j, value in zip(which, column_sweep(which)):
+                value = jnp.sum(value, axis=0, keepdims=True)
                 cbuf[step, c, r, :, lane(j - which[0])] = value
             send_columns(step, c)
 
     def row_pass(step):
-        take_columns(step, 0)
-        row_sweep(0, 0)
-        row_sweep(1, 0)
-        take_columns(step, 1)
-        for h in range(2):
-            row_sweep(h, 1)
-
-            def store(at, value):
-                rbuf[step, h, p, :, at] = value
-
-            lane_sums(acc, store, range(h * groups // 2, (h + 1) * groups // 2))
-            send_sums(step, h)
+        for c in range(2):
+            take_columns(step, c)
+            row_sweep(c)
+
+        def store(at, value):
+            rbuf[step, p, :, at] = value
+
+        lane_sums(acc, store, range(groups))
+        send_sums(step)
 
     steps = protos // MIDDLE
 
@@ -305,6 +296,20 @@
     for c in range(2):
         kernel_half(1 - lax.div(y, 2), c, False)
         send_columns(0, c)
+
+    chips = [lax.rem(x + ahead, CHIPS) for ahead in (2, 1, 3, 0)]
+    places = [(0, 1), (0, 0), (1, 1), (2, 1), (1, 0), (2, 0), (3, 1), (3, 0)]
+    owners = [chips[k] * 2 + lax.rem(core + other, 2) for k, other in places]
+
+    def chunk_of(place):
+        return pl.ds(pl.multiple_of(owners[place] * chunk, chunk), chunk)
+
+    turns = [
+        pltpu.make_async_copy(
+            uw.at[chunk_of(k)], wv.at[pl.ds(k * chunk, chunk)], turn_sem.at[k]
+        )
+        for k in range(n_rows)
+    ]
 
     for step in range(PASSES):
         if step > 0:
@@ -318,34 +323,54 @@
         if step == 0:
             student_begin()
         elif step == 1:
+            for copy in turns:
+                copy.start()
             st[...] = jnp.transpose(sg[...].reshape(rows, depth).astype(f32)).astype(bf16)
-    for h in range(2):
-        take_sums(PASSES - 1, h)
-
-    def delta(owner):
-        at = pl.ds(pl.multiple_of(owner * chunk, chunk), chunk)
+    take_sums(PASSES - 1)
+
+    def send(source, target, send_sem, recv_sem, to):
+        remote(source, target, send_sem, recv_sem, {"rows": to})
+
+    up = lax.rem(x + 1, CHIPS) * 2 + core
+    down = lax.rem(x + CHIPS - 1, CHIPS) * 2 + core
+    mate = x * 2 + 1 - core
+
+    def delta(place):
+        at = chunk_of(place)
+        to = slice(place * chunk, (place + 1) * chunk)
         cols = cvec[:, at]
-
-        def one(i, _):
-            here = pl.ds(pl.multiple_of(i * 16, 16), 16)
+        for i in range(rows // 16):
+            here = slice(i * 16, (i + 1) * 16)
             row = jnp.concatenate([rb[here, :]] * (chunk // LANES), axis=1)
             inv = jnp.concatenate([qb[here, :]] * (chunk // LANES), axis=1)
             value = pm[here, at] * inv - km[here, at] * row * cols
-            dall[here, at] = value.astype(bf16)
-            return 0
-
-        lax.fori_loop(0, rows // 16, one, 0, unroll=2)
-
-    def term(owner):
-        at = pl.ds(pl.multiple_of(owner * chunk, chunk), chunk)
-        return jnp.dot(st[...], dall[:, at], preferred_element_type=f32)
+            dall[here, to] = value.astype(bf16)
+
+    def term(place, following=None):
+        part = jnp.dot(
+            st[...], dall[:, place * chunk:(place + 1) * chunk], preferred_element_type=f32
+        )
+        if following is not None:
+            delta(following)
+        k, other = places[place]
+        if other:
+            psend[k, 0] = part[:, :half].astype(bf16)
+            psend[k, 1] = part[:, half:].astype(bf16)
+            for h in range(2):
+                send(psend.at[k, h], precv.at[k, h], p_ss.at[k, h], p_rs.at[k, h], mate)
+        else:
+            pown[k, 0] = part[:, :half]
+            pown[k, 1] = part[:, half:]
+
+    def joined(k, h):
+        return pown[k, h] + precv[k, h].astype(f32)
 
     def features():
         half_rows = rows // 2
 
         def one(i, _):
             here = pl.ds(pl.multiple_of(i * half_rows, half_rows), half_rows)
-            part = jnp.dot(dall[here, :], uw[...], preferred_element_type=f32).astype(bf16)
+            part = jnp.dot(dall[here, :], wv[...], preferred_element_type=f32).astype(bf16)
             to = pl.ds(i * (n_protos // 2), n_protos // 2)
             fsend[to] = part.reshape(n_protos // 2, block, depth)
             return 0
@@ -381,63 +406,39 @@
         one(depth_z - 1, 0)
         frecv[z] = fout[depth_z - 1]
 
-    def send(source, target, send_sem, recv_sem, to):
-        remote(source, target, send_sem, recv_sem, {"rows": to})
-
-    up = lax.rem(x + 1, CHIPS) * 2 + core
-    down = lax.rem(x + CHIPS - 1, CHIPS) * 2 + core
-    mate = x * 2 + 1 - core
-
-    chips = [lax.rem(x + ahead, CHIPS) for ahead in (2, 1, 3, 0)]
-
-    def to_mate(k):
-        part = term(chips[k] * 2 + 1 - core)
-        psend[k, 0] = part[:, :half].astype(bf16)
-        psend[k, 1] = part[:, half:].astype(bf16)
-        send(psend.at[k], precv.at[k], p_ss.at[k], p_rs.at[k], mate)
-
-    def with_mate(k):
-        part = term(chips[k] * 2 + core)
-        drain(precv.at[k], p_rs.at[k])
-        return part[:, :half] + precv[k, 0].astype(f32), part[:, half:] + precv[k, 1].astype(f32)
-
-    delta(chips[0] * 2 + 1 - core)
-    to_mate(0)
-    delta(chips[0] * 2 + core)
-    low, high = with_mate(0)
-    xsend[0, 0] = low.astype(bf16)
-    xsend[0, 1] = high.astype(bf16)
-    send(xsend.at[0, 0], relay.at[0], x_ss.at[0, 0], l_rs.at[0], up)
-    send(xsend.at[0, 1], relay.at[1], x_ss.at[0, 1], l_rs.at[1], down)
-    def deltas(k):
-        delta(chips[k] * 2 + 1 - core)
-        delta(chips[k] * 2 + core)
-
-    deltas(1)
-    to_mate(1)
-    deltas(2)
-    to_mate(2)
-    low, high = with_mate(1)
-    hold[0] = low
-    xsend[1, 1] = high.astype(bf16)
-    send(xsend.at[1, 1], xrecv.at[0, 1], x_ss.at[1, 1], x_rs.at[0, 1], up)
-    low, high = with_mate(2)
-    hold[1] = high
-    xsend[2, 0] = low.astype(bf16)
-    send(xsend.at[2, 0], xrecv.at[1, 0], x_ss.at[2, 0], x_rs.at[1, 0], down)
-    deltas(3)
+    delta(0)
+    for h in range(2):
+        part = jnp.dot(
+            st[...], dall[:, h * half:(h + 1) * half], preferred_element_type=f32
+        )
+        psend[0, h] = part.astype(bf16)
+        send(psend.at[0, h], precv.at[0, h], p_ss.at[0, h], p_rs.at[0, h], mate)
+        if h == 0:
+            delta(1)
+    term(1, 2)
+    term(2, 3)
+    for h, to in ((0, up), (1, down)):
+        drain(precv.at[0, h], p_rs.at[0, h])
+        xsend[0, h] = joined(0, h).astype(bf16)
+        send(xsend.at[0, h], relay.at[h], x_ss.at[0, h], l_rs.at[h], to)
+        if h == 0:
+            term(3, 4)
+    term(4, 5)
+    term(5, 6)
+    for k, h, to in ((1, 1, up), (2, 0, down)):
+        drain(precv.at[k, h], p_rs.at[k, h])
+        xsend[k, h] = joined(k, h).astype(bf16)
+        send(xsend.at[k, h], xrecv.at[k - 1, h], x_ss.at[k, h], x_rs.at[k - 1, h], to)
+    term(6, 7)
+    for copy in turns:
+        copy.wait()
     features()
-    to_mate(3)
-    low, high = with_mate(3)
-    own[0] = low
-    own[1] = high
-
-    drain(relay.at[0], l_rs.at[0])
-    xsend[1, 0] = (hold[0] + relay[0].astype(f32)).astype(bf16)
-    send(xsend.at[1, 0], xrecv.at[0, 0], x_ss.at[1, 0], x_rs.at[0, 0], up)
-    drain(relay.at[1], l_rs.at[1])
-    xsend[2, 1] = (hold[1] + relay[1].astype(f32)).astype(bf16)
-    send(xsend.at[2, 1], xrecv.at[1, 1], x_ss.at[2, 1], x_rs.at[1, 1], down)
+    term(7)
+    for k, h, to in ((1, 0, up), (2, 1, down)):
+        drain(precv.at[k, h], p_rs.at[k, h])
+        drain(relay.at[h], l_rs.at[h])
+        xsend[k, h] = (joined(k, h) + relay[h].astype(f32)).astype(bf16)
+        send(xsend.at[k, h], xrecv.at[k - 1, h], x_ss.at[k, h], x_rs.at[k - 1, h], to)
 
     features_on()
     drain(frecv.at[pl.ds(0, depth_z - 1)], f_rs)
@@ -445,11 +446,13 @@
     total = lax.fori_loop(0, depth_z, lambda i, a: a + frecv[i].astype(f32), total)
     fg_ref[...] = scale * total
 
+    for h in range(2):
+        drain(precv.at[3, h], p_rs.at[3, h])
     for side in range(2):
         for h in range(2):
             drain(xrecv.at[side, h], x_rs.at[side, h])
     for h in range(2):
-        whole = own[h] + xrecv[0, h].astype(f32) + xrecv[1, h].astype(f32)
+        whole = joined(3, h) + xrecv[0, h].astype(f32) + xrecv[1, h].astype(f32)
         pg_ref[h * half:(h + 1) * half, :] = jnp.transpose(factor * whole)
 
     drain(tg.at[others], t_ss)
@@ -460,9 +463,10 @@
     for step in range(PASSES):
         for h in range(2):
             drain(cbuf.at[step, h, pl.ds(0, n_rows - 1)], c_ss.at[step, h])
-            drain(rbuf.at[step, h, others], r_ss.at[step, h])
+        drain(rbuf.at[step, others], r_ss.at[step])
     for k in range(4):
-        drain(psend.at[k], p_ss.at[k])
+        for h in range(2):
+            drain(psend.at[k, h], p_ss.at[k, h])
     for k in range(3):
         for h in range(2):
             drain(xsend.at[k, h], x_ss.at[k, h])
@@ -507,10 +511,9 @@
             vmem((rows, LANES), f32),
             vmem((rows, LANES), f32),
             vmem((rows, LANES), f32),
-            vmem((8, protos), f32),
             vmem((PASSES, 2, n_rows, 1, protos // 2), f32),
             vmem((1, protos), f32),
-            vmem((PASSES, 2, n_protos, 1, rows // 2), f32),
+            vmem((PASSES, n_protos, 1, rows), f32),
             vmem((n_protos, 1, rows), f32),
             vmem((protos, depth), bf16),
             vmem((block, depth), bf16),
@@ -525,18 +528,17 @@
             vmem((3, 2, depth, half), bf16),
             vmem((2, depth, half), bf16),
             vmem((2, 2, depth, half), bf16),
-            vmem((2, depth, half), f32),
-            vmem((2, depth, half), f32),
-            dma((3,)), dma, dma((depth_z - 1,)), dma((LINES - 1,)),
+            vmem((4, 2, depth, half), f32),
+            dma((3,)), dma((n_rows,)), dma, dma((depth_z - 1,)), dma((LINES - 1,)),
             dma, dma((depth_z - 1,)), dma((LINES - 1,)),
-            dma((PASSES, 2)), dma((PASSES, 2)), dma((PASSES, 2)), dma((PASSES, 2)),
+            dma((PASSES, 2)), dma((PASSES, 2)), dma((PASSES,)), dma((PASSES,)),
             dma, dma,
-            dma((4,)), dma((4,)),
+            dma((4, 2)), dma((4, 2)),
             dma((3, 2)), dma((2,)), dma((2, 2)),
             dma, dma((depth_z,)), dma, dma,
         ],
         compiler_params=pltpu.CompilerParams(
-            collective_id=0, has_side_effects=True, vmem_limit_bytes=42 * 1024 * 1024
+            collective_id=0, has_side_effects=True, vmem_limit_bytes=46 * 1024 * 1024
         ),
         name="head_step",
     )(*(pltpu.with_memory_space_constraint(v, pltpu.HBM) for v in (teacher_features, student_features, prototypes)))

time: 77.9 us -> 74.6 us (0.958)
  Pallas kernels: 77.1 us -> 73.8 us
    pallas_call x1, Pallas kernels: 76.2 us -> 72.9 us  [on_device(): pl.pallas_call(functools.partial(kernel, n_rows, n_protos, rows * n_rows)...]
where the time goes in v4:
time: 74.6 us; the launch traced here: 74.4 us
  Pallas kernels  73.8 us (99%)
    pallas_call x1, Pallas kernels, on_device(): pl.pallas_call(functools.partial(kernel, n_rows, n_protos, rows * n_rows)...  72.9 us

profile of v4, /device:TPU:1, one launch (start us, length us, event | category | flops | bytes accessed | tf_op | source)
XLA Modules:
  0.0 74.4 jit_solution(2351160925257093233)
XLA Ops:
  0.6 72.9 %head_step.1 = (f32[16,384]{1,0:T(8,128)S(1)}, f32[512,384]{1,0:T(8,128)S(1)}) custom-call(bf16[16,384]{1,0:T(8,128)(2,1)} %t_hbm.1, bf16[16,384]{1,0:T(8,128)(2,1)} %s_hbm.1, bf16[4096,384]{1,0:T(8,128)(2,1)} %w_ref.1), custom_call_target="tpu_custom_call" | custom-call | tf_op jit(solution)/shard_map/head_step/pallas_call | solution.py:496
  73.5 0.9 %store.1 = (f32[16,384]{1,0:T(8,128)}, f32[512,384]{1,0:T(8,128)}) custom-call(f32[16,384]{1,0:T(8,128)S(1)} %get-tuple-element.6.feature, f32[512,384]{1,0:T(8,128)S(1)} %get-tuple-element.7.proto), custom_call_target="tpu_custom_call" | custom-call | tf_op jit(solution)/shard_map/store/pallas_call | solution.py:545

commit v5 on v4

--- a/solution.py
+++ b/solution.py
@@ -13,7 +13,7 @@
 EPS = 1e-06
 LANES = 128
 STEP = 256
-WIDE = 1024
+WIDE = 2048
 MIDDLE = 512
 CHIPS = 4
 LINES = 4
@@ -31,7 +31,7 @@
     n_rows, n_protos, factor_rows,
     t_hbm, s_hbm, w_ref, fg_ref, pg_ref,
     tg, sg, uw, km, pm, st, rb, qb, acc, cbuf, cvec, rbuf, qbuf,
-    wv, t_ref, s_ref, dall, fsend, fline, fout, frecv, psend, precv, xsend, relay, xrecv, pown,
+    wv, t_ref, s_ref, dall, fsend, fline, fout, frecv, psend, precv, xsend, xnear, relay, xrecv, pown,
     in_sem, turn_sem, t_ss, tz_rs, ty_rs, s_ss, sz_rs, sy_rs, c_ss, c_rs, r_ss, r_rs, q_ss, q_rs,
     p_ss, p_rs, x_ss, l_rs, x_rs, f_ss, fy_rs, g_ss, f_rs,
 ):
@@ -105,7 +105,7 @@
     pl.semaphore_wait(barrier, depth_z + LINES + n_rows - 3)
 
     def along_z(buf, send_sem, recv_sem):
-        for j in range(depth_z - 1):
+        for j in reversed(range(depth_z - 1)):
             dz = depth_z // 2 + (j + 1) // 2 * (1 - 2 * (j % 2))
             remote(
                 buf.at[p], buf.at[p], send_sem, recv_sem.at[dz - 1], {"protos": spot(0, dz)}
@@ -117,20 +117,18 @@
             remote(buf.at[q], buf.at[q], send_sem, recv_sem.at[dy - 1], {"protos": to})
 
     def pass_on(buf, send_sem, z_sem, y_sem):
-        along_y(buf, p, send_sem, y_sem, (1, 3))
         for j in reversed(range(depth_z - 1)):
             dz = depth_z // 2 + (j + 1) // 2 * (1 - 2 * (j % 2))
             q = spot(0, depth_z - dz)
             drain(buf.at[q], z_sem.at[dz - 1])
-            along_y(buf, q, send_sem, y_sem, (1, 3))
-        for k in range(depth_z):
-            along_y(buf, y * depth_z + k, send_sem, y_sem, (2,))
+            along_y(buf, q, send_sem, y_sem, (1, 3, 2))
 
     def column_here(buf, dy, y_sem):
         line = lax.rem(y + LINES - dy, LINES) * depth_z
         drain(buf.at[pl.ds(line, depth_z)], y_sem.at[dy - 1])
 
     along_z(tg, t_ss, tz_rs)
+    along_y(tg, p, t_ss, ty_rs, (1, 3, 2))
     along_z(sg, s_ss, sz_rs)
     loads[2].wait()
 
@@ -174,6 +172,7 @@
     drain(tg.at[pl.ds(line, depth_z)], ty_rs.at[near - 1])
     kernel_half(lax.div(y, 2), 0, True)
     kernel_half(lax.div(y, 2), 1, True)
+    along_y(sg, p, s_ss, sy_rs, (1, 3, 2))
     pass_on(sg, s_ss, sz_rs, sy_rs)
     line = lax.rem(y + near, LINES) * depth_z
     drain(tg.at[pl.ds(line, depth_z)], ty_rs.at[LINES - near - 1])
@@ -226,6 +225,19 @@
             return 0
 
         lax.fori_loop(0, rows // 8, one, 0, unroll=4)
+
+    def scale_both():
+        cols = [jnp.broadcast_to(cvec[:, lane(j)], (8, LANES)) for j in range(tiles)]
+
+        def one(i, _):
+            at = rows_of(i)
+            value = qb[at, :]
+            for j in range(tiles):
+                pm[at, lane(j)] = pm[at, lane(j)] * value
+                km[at, lane(j)] = km[at, lane(j)] * cols[j]
+            return 0
+
+        lax.fori_loop(0, rows // 8, one, 0, unroll=2)
 
     def send_columns(step, c):
         mine = cbuf.at[step, c, r]
@@ -326,6 +338,7 @@
             for copy in turns:
                 copy.start()
             st[...] = jnp.transpose(sg[...].reshape(rows, depth).astype(f32)).astype(bf16)
+    scale_both()
     take_sums(PASSES - 1)
 
     def send(source, target, send_sem, recv_sem, to):
@@ -338,12 +351,10 @@
     def delta(place):
         at = chunk_of(place)
         to = slice(place * chunk, (place + 1) * chunk)
-        cols = cvec[:, at]
         for i in range(rows // 16):
             here = slice(i * 16, (i + 1) * 16)
             row = jnp.concatenate([rb[here, :]] * (chunk // LANES), axis=1)
-            inv = jnp.concatenate([qb[here, :]] * (chunk // LANES), axis=1)
-            value = pm[here, at] * inv - km[here, at] * row * cols
+            value = pm[here, at] - km[here, at] * row
             dall[here, to] = value.astype(bf16)
 
     def term(place, following=None):
@@ -419,16 +430,16 @@
     term(2, 3)
     for h, to in ((0, up), (1, down)):
         drain(precv.at[0, h], p_rs.at[0, h])
-        xsend[0, h] = joined(0, h).astype(bf16)
-        send(xsend.at[0, h], relay.at[h], x_ss.at[0, h], l_rs.at[h], to)
+        xsend[h] = joined(0, h).astype(bf16)
+        send(xsend.at[h], relay.at[h], x_ss.at[0, h], l_rs.at[h], to)
         if h == 0:
             term(3, 4)
     term(4, 5)
     term(5, 6)
     for k, h, to in ((1, 1, up), (2, 0, down)):
         drain(precv.at[k, h], p_rs.at[k, h])
-        xsend[k, h] = joined(k, h).astype(bf16)
-        send(xsend.at[k, h], xrecv.at[k - 1, h], x_ss.at[k, h], x_rs.at[k - 1, h], to)
+        xnear[k - 1, h] = jnp.transpose(joined(k, h)).astype(bf16)
+        send(xnear.at[k - 1, h], xrecv.at[k - 1, h], x_ss.at[k, h], x_rs.at[k - 1, h], to)
     term(6, 7)
     for copy in turns:
         copy.wait()
@@ -437,39 +448,42 @@
     for k, h, to in ((1, 0, up), (2, 1, down)):
         drain(precv.at[k, h], p_rs.at[k, h])
         drain(relay.at[h], l_rs.at[h])
-        xsend[k, h] = (joined(k, h) + relay[h].astype(f32)).astype(bf16)
-        send(xsend.at[k, h], xrecv.at[k - 1, h], x_ss.at[k, h], x_rs.at[k - 1, h], to)
+        xnear[k - 1, h] = jnp.transpose(joined(k, h) + relay[h].astype(f32)).astype(bf16)
+        send(xnear.at[k - 1, h], xrecv.at[k - 1, h], x_ss.at[k, h], x_rs.at[k - 1, h], to)
 
     features_on()
+    for h in range(2):
+        drain(precv.at[3, h], p_rs.at[3, h])
+        pg_ref[h * half:(h + 1) * half, :] = jnp.transpose(joined(3, h))
+
+    drain(tg.at[others], t_ss)
+    drain(sg.at[others], s_ss)
+    drain(qbuf.at[others], q_ss)
+    for step in range(PASSES):
+        for h in range(2):
+            drain(cbuf.at[step, h, pl.ds(0, n_rows - 1)], c_ss.at[step, h])
+        drain(rbuf.at[step, others], r_ss.at[step])
+    for h in range(2):
+        for k in range(4):
+            drain(psend.at[k, h], p_ss.at[k, h])
+        drain(xsend.at[h], x_ss.at[0, h])
+    drain(fline, f_ss)
+
     drain(frecv.at[pl.ds(0, depth_z - 1)], f_rs)
     total = jnp.zeros((block, depth), f32)
     total = lax.fori_loop(0, depth_z, lambda i, a: a + frecv[i].astype(f32), total)
     fg_ref[...] = scale * total
+    drain(frecv.at[pl.ds(0, depth_z - 1)], g_ss)
 
     for h in range(2):
-        drain(precv.at[3, h], p_rs.at[3, h])
-    for side in range(2):
+        for line in range(2):
+            drain(xrecv.at[line, h], x_rs.at[line, h])
+    here = slice(0, chunk)
+    received = [xrecv[line].reshape(chunk, depth).astype(f32) for line in range(2)]
+    pg_ref[here, :] = factor * (pg_ref[here, :] + (received[0] + received[1]))
+    for k in range(2):
         for h in range(2):
-            drain(xrecv.at[side, h], x_rs.at[side, h])
-    for h in range(2):
-        whole = joined(3, h) + xrecv[0, h].astype(f32) + xrecv[1, h].astype(f32)
-        pg_ref[h * half:(h + 1) * half, :] = jnp.transpose(factor * whole)
-
-    drain(tg.at[others], t_ss)
-    drain(sg.at[others], s_ss)
-    drain(qbuf.at[others], q_ss)
-    drain(fline, f_ss)
-    drain(frecv.at[pl.ds(0, depth_z - 1)], g_ss)
-    for step in range(PASSES):
-        for h in range(2):
-            drain(cbuf.at[step, h, pl.ds(0, n_rows - 1)], c_ss.at[step, h])
-        drain(rbuf.at[step, others], r_ss.at[step])
-    for k in range(4):
-        for h in range(2):
-            drain(psend.at[k, h], p_ss.at[k, h])
-    for k in range(3):
-        for h in range(2):
-            drain(xsend.at[k, h], x_ss.at[k, h])
+            drain(xnear.at[k, h], x_ss.at[k + 1, h])
 
 
 def store(feature, proto, feature_out, proto_out, f_sem, p_sem):
@@ -525,9 +539,10 @@
             vmem((depth_z, block, depth), bf16),
             vmem((4, 2, depth, half), bf16),
             vmem((4, 2, depth, half), bf16),
-            vmem((3, 2, depth, half), bf16),
             vmem((2, depth, half), bf16),
-            vmem((2, 2, depth, half), bf16),
+            vmem((2, 2, half, depth), bf16),
+            vmem((2, depth, half), bf16),
+            vmem((2, 2, half, depth), bf16),
             vmem((4, 2, depth, half), f32),
             dma((3,)), dma((n_rows,)), dma, dma((depth_z - 1,)), dma((LINES - 1,)),
             dma, dma((depth_z - 1,)), dma((LINES - 1,)),

time: 74.6 us -> 73.7 us (0.988)
  Pallas kernels: 73.8 us -> 73 us
    pallas_call x1, Pallas kernels: 72.9 us -> 72.1 us  [on_device(): pl.pallas_call(functools.partial(kernel, n_rows, n_protos, rows * n_rows)...]
where the time goes in v5:
time: 73.7 us; the launch traced here: 73.6 us
  Pallas kernels  73 us (99%)
    pallas_call x1, Pallas kernels, on_device(): pl.pallas_call(functools.partial(kernel, n_rows, n_protos, rows * n_rows)...  72.1 us

profile of v5, /device:TPU:1, one launch (start us, length us, event | category | flops | bytes accessed | tf_op | source)
XLA Modules:
  0.0 73.6 jit_solution(9602027487235806649)
XLA Ops:
  0.6 72.1 %head_step.1 = (f32[16,384]{1,0:T(8,128)S(1)}, f32[512,384]{1,0:T(8,128)S(1)}) custom-call(bf16[16,384]{1,0:T(8,128)(2,1)} %t_hbm.1, bf16[16,384]{1,0:T(8,128)(2,1)} %s_hbm.1, bf16[4096,384]{1,0:T(8,128)(2,1)} %w_ref.1), custom_call_target="tpu_custom_call" | custom-call | tf_op jit(solution)/shard_map/head_step/pallas_call | solution.py:510
  72.7 0.9 %store.1 = (f32[16,384]{1,0:T(8,128)}, f32[512,384]{1,0:T(8,128)}) custom-call(f32[16,384]{1,0:T(8,128)S(1)} %get-tuple-element.6.feature, f32[512,384]{1,0:T(8,128)S(1)} %get-tuple-element.7.proto), custom_call_target="tpu_custom_call" | custom-call | tf_op jit(solution)/shard_map/store/pallas_call | solution.py:560

commit v6 on v5

--- a/solution.py
+++ b/solution.py
@@ -129,7 +129,6 @@
 
     along_z(tg, t_ss, tz_rs)
     along_y(tg, p, t_ss, ty_rs, (1, 3, 2))
-    along_z(sg, s_ss, sz_rs)
     loads[2].wait()
 
     def unit_step(i, _):
@@ -141,6 +140,7 @@
 
     others = pl.ds(0, n_protos - 1)
     pass_on(tg, t_ss, tz_rs, ty_rs)
+    along_z(sg, s_ss, sz_rs)
     def logits(left, i, width):
         at = pl.ds(pl.multiple_of(i * width, width), width)
         values = lax.dot_general(
@@ -172,8 +172,6 @@
     drain(tg.at[pl.ds(line, depth_z)], ty_rs.at[near - 1])
     kernel_half(lax.div(y, 2), 0, True)
     kernel_half(lax.div(y, 2), 1, True)
-    along_y(sg, p, s_ss, sy_rs, (1, 3, 2))
-    pass_on(sg, s_ss, sz_rs, sy_rs)
     line = lax.rem(y + near, LINES) * depth_z
     drain(tg.at[pl.ds(line, depth_z)], ty_rs.at[LINES - near - 1])
     column_here(tg, 2, ty_rs)
@@ -309,6 +307,9 @@
         kernel_half(1 - lax.div(y, 2), c, False)
         send_columns(0, c)
 
+    along_y(sg, p, s_ss, sy_rs, (1, 3, 2))
+    pass_on(sg, s_ss, sz_rs, sy_rs)
+
     chips = [lax.rem(x + ahead, CHIPS) for ahead in (2, 1, 3, 0)]
     places = [(0, 1), (0, 0), (1, 1), (2, 1), (1, 0), (2, 0), (3, 1), (3, 0)]
     owners = [chips[k] * 2 + lax.rem(core + other, 2) for k, other in places]
@@ -326,19 +327,18 @@
     for step in range(PASSES):
         if step > 0:
             column_pass(step)
-        if step == 1:
-            student_end()
-        elif step == 2:
-            drain(qbuf.at[others], q_rs)
-            to_columns(1.0 / jnp.sum(qbuf[...], axis=0), qb)
         row_pass(step)
         if step == 0:
             student_begin()
+            st[...] = jnp.transpose(sg[...].reshape(rows, depth).astype(f32)).astype(bf16)
         elif step == 1:
+            student_end()
+        else:
+            drain(qbuf.at[others], q_rs)
+            to_columns(1.0 / jnp.sum(qbuf[...], axis=0), qb)
+            scale_both()
             for copy in turns:
                 copy.start()
-            st[...] = jnp.transpose(sg[...].reshape(rows, depth).astype(f32)).astype(bf16)
-    scale_both()
     take_sums(PASSES - 1)
 
     def send(source, target, send_sem, recv_sem, to):

time: 73.7 us -> 73 us (level)
  Pallas kernels: 73 us -> 72.2 us
    pallas_call x1, Pallas kernels: 72.1 us -> 71.3 us  [on_device(): pl.pallas_call(functools.partial(kernel, n_rows, n_protos, rows * n_rows)...]
where the time goes in v6:
time: 73 us; the launch traced here: 72.8 us
  Pallas kernels  72.2 us (99%)
    pallas_call x1, Pallas kernels, on_device(): pl.pallas_call(functools.partial(kernel, n_rows, n_protos, rows * n_rows)...  71.3 us

profile of v6, /device:TPU:1, one launch (start us, length us, event | category | flops | bytes accessed | tf_op | source)
XLA Modules:
  0.0 72.8 jit_solution(10375485238375929116)
XLA Ops:
  0.6 71.3 %head_step.1 = (f32[16,384]{1,0:T(8,128)S(1)}, f32[512,384]{1,0:T(8,128)S(1)}) custom-call(bf16[16,384]{1,0:T(8,128)(2,1)} %t_hbm.1, bf16[16,384]{1,0:T(8,128)(2,1)} %s_hbm.1, bf16[4096,384]{1,0:T(8,128)(2,1)} %w_ref.1), custom_call_target="tpu_custom_call" | custom-call | tf_op jit(solution)/shard_map/head_step/pallas_call | solution.py:510
  71.9 0.9 %store.1 = (f32[16,384]{1,0:T(8,128)}, f32[512,384]{1,0:T(8,128)}) custom-call(f32[16,384]{1,0:T(8,128)S(1)} %get-tuple-element.6.feature, f32[512,384]{1,0:T(8,128)S(1)} %get-tuple-element.7.proto), custom_call_target="tpu_custom_call" | custom-call | tf_op jit(solution)/shard_map/store/pallas_call | solution.py:560

commit v7 on v6

--- a/solution.py
+++ b/solution.py
@@ -200,29 +200,27 @@
         return pl.ds(pl.multiple_of(i * 8, 8), 8)
 
     def column_sweep(which):
-        def one(i, sums):
-            at = rows_of(i)
+        sums = [jnp.zeros((8, LANES), f32) for _ in which]
+        for i in range(rows // 8):
+            at = slice(i * 8, (i + 1) * 8)
             value = rb[at, :]
-            return tuple(s + km[at, lane(j)] * value for s, j in zip(sums, which))
-
-        return lax.fori_loop(
-            0, rows // 8, one, tuple(jnp.zeros((8, LANES), f32) for _ in which), unroll=4
-        )
+            sums = [s + km[at, lane(j)] * value for s, j in zip(sums, which)]
+        return sums
 
     def row_sweep(c):
         which = range(c * tiles // 2, (c + 1) * tiles // 2)
         cols = [jnp.broadcast_to(cvec[:, lane(j)], (8, LANES)) for j in which]
 
-        def one(i, _):
-            at = rows_of(i)
+        def one(i):
+            at = slice(i * 8, (i + 1) * 8)
             parts = [km[at, lane(j)] * col for j, col in zip(which[:4], cols[:4])]
             for k in range(4, len(which)):
                 parts[k % 4] = parts[k % 4] + km[at, lane(which[k])] * cols[k]
             total = (parts[0] + parts[1]) + (parts[2] + parts[3])
             acc[at, :] = total if c == 0 else acc[at, :] + total
-            return 0
-
-        lax.fori_loop(0, rows // 8, one, 0, unroll=4)
+
+        for i in range(rows // 8):
+            one(i)
 
     def scale_both():
         cols = [jnp.broadcast_to(cvec[:, lane(j)], (8, LANES)) for j in range(tiles)]
@@ -348,12 +346,13 @@
     down = lax.rem(x + CHIPS - 1, CHIPS) * 2 + core
     mate = x * 2 + 1 - core
 
-    def delta(place):
-        at = chunk_of(place)
-        to = slice(place * chunk, (place + 1) * chunk)
-        for i in range(rows // 16):
+    def delta(place, parts=range(rows // 16), columns=slice(0, chunk)):
+        width = columns.stop - columns.start
+        at = pl.ds(pl.multiple_of(owners[place] * chunk + columns.start, width), width)
+        to = slice(place * chunk + columns.start, place * chunk + columns.stop)
+        for i in parts:
             here = slice(i * 16, (i + 1) * 16)
-            row = jnp.concatenate([rb[here, :]] * (chunk // LANES), axis=1)
+            row = jnp.concatenate([rb[here, :]] * (width // LANES), axis=1)
             value = pm[here, at] - km[here, at] * row
             dall[here, to] = value.astype(bf16)
 
@@ -417,23 +416,29 @@
         one(depth_z - 1, 0)
         frecv[z] = fout[depth_z - 1]
 
-    delta(0)
-    for h in range(2):
+    def first_half(h):
         part = jnp.dot(
             st[...], dall[:, h * half:(h + 1) * half], preferred_element_type=f32
         )
         psend[0, h] = part.astype(bf16)
         send(psend.at[0, h], precv.at[0, h], p_ss.at[0, h], p_rs.at[0, h], mate)
-        if h == 0:
-            delta(1)
+
+    delta(0, range(rows // 16), slice(0, half))
+    first_half(0)
+
+    @pl.when(p >= 0)
+    def _():
+        delta(0, range(rows // 16), slice(half, chunk))
+        first_half(1)
+        delta(1)
+
     term(1, 2)
     term(2, 3)
     for h, to in ((0, up), (1, down)):
         drain(precv.at[0, h], p_rs.at[0, h])
         xsend[h] = joined(0, h).astype(bf16)
         send(xsend.at[h], relay.at[h], x_ss.at[0, h], l_rs.at[h], to)
-        if h == 0:
-            term(3, 4)
+    term(3, 4)
     term(4, 5)
     term(5, 6)
     for k, h, to in ((1, 1, up), (2, 0, down)):

time: 73 us -> 71.9 us (0.985)
  Pallas kernels: 72.2 us -> 70.9 us
    pallas_call x1, Pallas kernels: 71.3 us -> 70 us  [on_device(): pl.pallas_call(functools.partial(kernel, n_rows, n_protos, rows * n_rows)...]
where the time goes in v7:
time: 71.9 us; the launch traced here: 71.7 us
  Pallas kernels  70.9 us (99%)
  between operations  0.8 us (1%)
    pallas_call x1, Pallas kernels, on_device(): pl.pallas_call(functools.partial(kernel, n_rows, n_protos, rows * n_rows)...  70 us

profile of v7, /device:TPU:1, one launch (start us, length us, event | category | flops | bytes accessed | tf_op | source)
XLA Modules:
  0.0 71.7 jit_solution(15195230856807665202)
XLA Ops:
  0.6 70.0 %head_step.1 = (f32[16,384]{1,0:T(8,128)S(1)}, f32[512,384]{1,0:T(8,128)S(1)}) custom-call(bf16[16,384]{1,0:T(8,128)(2,1)} %t_hbm.1, bf16[16,384]{1,0:T(8,128)(2,1)} %s_hbm.1, bf16[4096,384]{1,0:T(8,128)(2,1)} %w_ref.1), custom_call_target="tpu_custom_call" | custom-call | tf_op jit(solution)/shard_map/head_step/pallas_call | solution.py:515
  70.7 0.9 %store.1 = (f32[16,384]{1,0:T(8,128)}, f32[512,384]{1,0:T(8,128)}) custom-call(f32[16,384]{1,0:T(8,128)S(1)} %get-tuple-element.6.feature, f32[512,384]{1,0:T(8,128)S(1)} %get-tuple-element.7.proto), custom_call_target="tpu_custom_call" | custom-call | tf_op jit(solution)/shard_map/store/pallas_call | solution.py:565
